TPU v7x, 32 devices: a whole 2x2x4 slice. The times are simulated.
32 devices in a mesh: dp: 8 (over y, x, core), ctx: 4 (over z).
Axes of the slice: x: 2, y: 2, z: 4, core: 2. Of those that a mesh axis runs over, the one named last changes fastest.
Arguments:
- tokens: bfloat16 [8, 512, 1088], P('dp', 'ctx'), may hold values from -32 to 32
- cotangent: bfloat16 [8, 512, 1088], P('dp', 'ctx'), may hold values from -6 to 6
- ln1_gain: float32 [1088], P('dp'), may hold values from 0.5 to 1.5
- ln1_bias: float32 [1088], P('dp'), may hold values from -1.5 to 1.5
- qkv_weight: bfloat16 [1088, 3264], P('dp'), may hold values from -10 to 10
- qv_bias: float32 [2, 1088], P(None, 'dp'), may hold values from -1.5 to 1.5
- out_weight: bfloat16 [1088, 1088], P('dp'), may hold values from -1.5 to 1.5
- out_bias: float32 [1088], P('dp'), may hold values from -1.5 to 1.5
- ln2_gain: float32 [1088], P('dp'), may hold values from 0.5 to 1.5
- ln2_bias: float32 [1088], P('dp'), may hold values from -1.5 to 1.5
- up_weight: bfloat16 [1088, 4352], P('dp'), may hold values from -0.1875 to 0.1875
- up_bias: float32 [4352], P('dp'), may hold values from -1.5 to 1.5
- down_weight: bfloat16 [4352, 1088], P('dp'), may hold values from -0.09375 to 0.09375
- down_bias: float32 [1088], P('dp'), may hold values from -1.5 to 1.5
Outputs:
- activations: bfloat16 [8, 512, 1088], P('dp', 'ctx')
- input_grad: bfloat16 [8, 512, 1088], P('dp', 'ctx')
- ln1_gain_grad: float32 [1088], P('dp')
- ln1_bias_grad: float32 [1088], P('dp')
- qkv_grad: float32 [1088, 3264], P('dp')
- qv_bias_grad: float32 [2, 1088], P(None, 'dp')
- out_grad: float32 [1088, 1088], P('dp')
- out_bias_grad: float32 [1088], P('dp')
- ln2_gain_grad: float32 [1088], P('dp')
- ln2_bias_grad: float32 [1088], P('dp')
- up_grad: float32 [1088, 4352], P('dp')
- up_bias_grad: float32 [4352], P('dp')
- down_grad: float32 [4352, 1088], P('dp')
- down_bias_grad: float32 [1088], P('dp')
All inputs are finite; a program needn't handle non-finite values.
Results may differ from a plain program's by a relative error of at most 0.012.
Values may be sent and summed in bfloat16 or wider, within the bound.
A program may use at most 192 MiB of HBM per device.

v0:
```python
import jax
import jax.numpy as jnp
from jax import lax
from jax.sharding import PartitionSpec as P

D = 1088
H = 17
HD = 64


EPSILON = 1e-05
ROOT_HALF = 0.7071067811865476
INV_ROOT_TAU = 0.3989422804014327


def norm_parts(values, norm_gain, norm_shift):
    average = jnp.mean(values, axis=-1, keepdims=True)
    centered = values - average
    inverse = lax.rsqrt(jnp.mean(centered * centered, axis=-1, keepdims=True) + EPSILON)
    normed = centered * inverse
    return (normed, inverse, normed * norm_gain + norm_shift)


def norm_back(grad_out, normed, inverse, norm_gain):
    scaled = grad_out * norm_gain
    return inverse * (
        scaled
        - jnp.mean(scaled, axis=-1, keepdims=True)
        - normed * jnp.mean(scaled * normed, axis=-1, keepdims=True)
    )


def gelu_exact(pre_act):
    return 0.5 * pre_act * (1.0 + lax.erf(pre_act * ROOT_HALF))


def gelu_slope(pre_act):
    return (
        0.5 * (1.0 + lax.erf(pre_act * ROOT_HALF))
        + pre_act * jnp.exp(-0.5 * pre_act * pre_act) * INV_ROOT_TAU
    )


def heads_first(matrix):
    return matrix.reshape(matrix.shape[0], H, HD).transpose(1, 0, 2)


def heads_last(stacked):
    return stacked.transpose(1, 0, 2).reshape(stacked.shape[1], H * HD)


def add_product(left_rows, block_rows):
    return jnp.dot(left_rows, block_rows, preferred_element_type=jnp.float32)


def project(inputs, weight):
    return add_product(inputs, lax.all_gather(weight, "dp", axis=0, tiled=True))


def project_back(grads_low, weight):
    return lax.dot_general(
        grads_low,
        lax.all_gather(weight, "dp", axis=0, tiled=True),
        (((1,), (1,)), ((), ())),
        preferred_element_type=jnp.float32,
    )


def weight_grad(inputs, grads_low):
    return lax.psum_scatter(
        lax.dot_general(
            inputs, grads_low, (((0,), (0,)), ((), ())), preferred_element_type=jnp.float32
        ),
        "dp",
        scatter_dimension=0,
        tiled=True,
    )


def head_scores(query_head, key_head, query_pos, key_pos):
    scores = lax.dot_general(
        query_head, key_head, (((1,), (1,)), ((), ())), preferred_element_type=jnp.float32
    ) * float(HD) ** (-0.5)
    allowed = key_pos[None, :] <= query_pos[:, None]
    return (jnp.where(allowed, scores, -1e30), allowed)


def attend(query_heads, key_heads, value_heads, query_pos, key_pos):

    def one_head(head_items):
        query_head, key_head, value_head = head_items
        scores, allowed = head_scores(query_head, key_head, query_pos, key_pos)
        highest = jnp.max(scores, axis=1, keepdims=True)
        summed = jnp.sum(jnp.where(allowed, jnp.exp(scores - highest), 0.0), axis=1, keepdims=True)
        log_total = highest + jnp.log(summed)
        probs_low = jnp.where(allowed, jnp.exp(scores - log_total), 0.0).astype(jnp.bfloat16)
        mixed = jnp.dot(probs_low, value_head, preferred_element_type=jnp.float32).astype(
            jnp.bfloat16
        )
        return (mixed, log_total[:, 0])

    return lax.map(one_head, (query_heads, key_heads, value_heads))


def score_grads(
    query_head, key_head, value_head, dout_head, log_total, delta_head, query_pos, key_pos
):
    scores, allowed = head_scores(query_head, key_head, query_pos, key_pos)
    probs_full = jnp.where(allowed, jnp.exp(scores - log_total[:, None]), 0.0)
    dprobs = lax.dot_general(
        dout_head, value_head, (((1,), (1,)), ((), ())), preferred_element_type=jnp.float32
    )
    dscores = (probs_full * (dprobs - delta_head[:, None])).astype(jnp.bfloat16)
    return (probs_full, dscores)


def per_device(
    tokens,
    cotangent,
    ln1_gain,
    ln1_bias,
    qkv_weight,
    qv_bias,
    out_weight,
    out_bias,
    ln2_gain,
    ln2_bias,
    up_weight,
    up_bias,
    down_weight,
    down_bias,
):
    scale = float(HD) ** (-0.5)
    local_count = tokens.shape[1]
    gathered = (
        lax.all_gather(ln1_gain, "dp", axis=0, tiled=True),
        lax.all_gather(ln1_bias, "dp", axis=0, tiled=True),
        lax.all_gather(qv_bias, "dp", axis=1, tiled=True),
        lax.all_gather(out_bias, "dp", axis=0, tiled=True),
        lax.all_gather(ln2_gain, "dp", axis=0, tiled=True),
        lax.all_gather(ln2_bias, "dp", axis=0, tiled=True),
        lax.all_gather(up_bias, "dp", axis=0, tiled=True),
        lax.all_gather(down_bias, "dp", axis=0, tiled=True),
    )
    gain_one, shift_one, bias_pair, bias_out, gain_two, shift_two, bias_up, bias_down = gathered
    inputs_full = tokens[0].astype(jnp.float32)
    normed_one, inverse_one, pre_one = norm_parts(inputs_full, gain_one, shift_one)
    act_one = pre_one.astype(jnp.bfloat16)
    mixed_qkv = project(act_one, qkv_weight)
    queries = (mixed_qkv[:, :D] + bias_pair[0]).astype(jnp.bfloat16)
    keys_low = mixed_qkv[:, D : 2 * D].astype(jnp.bfloat16)
    values_low = (mixed_qkv[:, 2 * D :] + bias_pair[1]).astype(jnp.bfloat16)
    all_keys, all_values = (
        lax.all_gather(keys_low, "ctx", axis=0, tiled=True),
        lax.all_gather(values_low, "ctx", axis=0, tiled=True),
    )
    query_pos = lax.axis_index("ctx") * local_count + jnp.arange(local_count)
    key_pos = jnp.arange(all_keys.shape[0])
    query_heads = heads_first(queries)
    kept_keys = heads_first(all_keys)
    kept_values = heads_first(all_values)
    mixed_heads, log_totals = attend(query_heads, kept_keys, kept_values, query_pos, key_pos)
    attended = heads_last(mixed_heads)
    hidden_one = inputs_full + (project(attended, out_weight) + bias_out)
    normed_two, inverse_two, pre_two = norm_parts(hidden_one, gain_two, shift_two)
    act_two = pre_two.astype(jnp.bfloat16)
    pre_up = project(act_two, up_weight) + bias_up
    activated = gelu_exact(pre_up).astype(jnp.bfloat16)
    output_full = hidden_one + (project(activated, down_weight) + bias_down)
    cot_low = cotangent[0]
    cot_full = cot_low.astype(jnp.float32)
    down_terms = weight_grad(activated, cot_low)
    dpre = project_back(cot_low, down_weight) * gelu_slope(pre_up)
    dpre_low = dpre.astype(jnp.bfloat16)
    up_terms = weight_grad(act_two, dpre_low)
    dnorm_two = project_back(dpre_low, up_weight)
    dhidden = cot_full + norm_back(dnorm_two, normed_two, inverse_two, gain_two)
    dhidden_low = dhidden.astype(jnp.bfloat16)
    out_terms = weight_grad(attended, dhidden_low)
    dattended = project_back(dhidden_low, out_weight).astype(jnp.bfloat16)
    dout_heads = heads_first(dattended)
    deltas = jnp.sum(dout_heads.astype(jnp.float32) * mixed_heads.astype(jnp.float32), axis=2)
    again_keys, again_values = (
        lax.all_gather(keys_low, "ctx", axis=0, tiled=True),
        lax.all_gather(values_low, "ctx", axis=0, tiled=True),
    )
    key_heads = heads_first(again_keys)
    value_heads = heads_first(again_values)

    def query_head_grad(head_items):
        query_head, key_head, value_head, dout_head, log_total, delta_head = head_items
        probs_full, dscores = score_grads(
            query_head, key_head, value_head, dout_head, log_total, delta_head, query_pos, key_pos
        )
        return jnp.dot(dscores, key_head, preferred_element_type=jnp.float32) * scale

    dqueries = heads_last(
        lax.map(
            query_head_grad, (query_heads, key_heads, value_heads, dout_heads, log_totals, deltas)
        )
    )
    block_pos = jnp.arange(lax.axis_size("ctx") * local_count)

    def key_head_grad(head_items):
        query_head, key_head, value_head, dout_head, log_total, delta_head = head_items
        probs_full, dscores = score_grads(
            query_head, key_head, value_head, dout_head, log_total, delta_head, query_pos, block_pos
        )
        probs_low = probs_full.astype(jnp.bfloat16)
        dkey = (
            lax.dot_general(
                dscores, query_head, (((0,), (0,)), ((), ())), preferred_element_type=jnp.float32
            )
            * scale
        )
        dvalue = lax.dot_general(
            probs_low, dout_head, (((0,), (0,)), ((), ())), preferred_element_type=jnp.float32
        )
        return (dkey, dvalue)

    dkey_heads, dvalue_heads = lax.map(
        key_head_grad, (query_heads, key_heads, value_heads, dout_heads, log_totals, deltas)
    )
    key_value_grads = lax.psum_scatter(
        jnp.concatenate([heads_last(dkey_heads), heads_last(dvalue_heads)], axis=1),
        "ctx",
        scatter_dimension=0,
        tiled=True,
    )
    dkeys = key_value_grads[:, :D]
    dvalues = key_value_grads[:, D:]
    dqkv = jnp.concatenate([dqueries, dkeys, dvalues], axis=1).astype(jnp.bfloat16)
    qkv_terms = weight_grad(act_one, dqkv)
    dnorm_one = project_back(dqkv, qkv_weight)
    input_grad = (dhidden + norm_back(dnorm_one, normed_one, inverse_one, gain_one)).astype(
        jnp.bfloat16
    )
    pair_sums = jnp.stack([jnp.sum(dqueries, axis=0), jnp.sum(dvalues, axis=0)])
    vector_shards = (
        lax.psum_scatter(
            jnp.sum(dnorm_one * normed_one, axis=0), "dp", scatter_dimension=0, tiled=True
        ),
        lax.psum_scatter(jnp.sum(dnorm_one, axis=0), "dp", scatter_dimension=0, tiled=True),
        lax.psum_scatter(pair_sums, "dp", scatter_dimension=1, tiled=True),
        lax.psum_scatter(jnp.sum(dhidden, axis=0), "dp", scatter_dimension=0, tiled=True),
        lax.psum_scatter(
            jnp.sum(dnorm_two * normed_two, axis=0), "dp", scatter_dimension=0, tiled=True
        ),
        lax.psum_scatter(jnp.sum(dnorm_two, axis=0), "dp", scatter_dimension=0, tiled=True),
        lax.psum_scatter(jnp.sum(dpre, axis=0), "dp", scatter_dimension=0, tiled=True),
        lax.psum_scatter(jnp.sum(cot_full, axis=0), "dp", scatter_dimension=0, tiled=True),
    )
    (
        gain_one_part,
        shift_one_part,
        pair_part,
        out_bias_part,
        gain_two_part,
        shift_two_part,
        up_bias_part,
        down_bias_part,
    ) = vector_shards
    totals = lax.psum(
        (
            gain_one_part,
            shift_one_part,
            qkv_terms,
            pair_part,
            out_terms,
            out_bias_part,
            gain_two_part,
            shift_two_part,
            up_terms,
            up_bias_part,
            down_terms,
            down_bias_part,
        ),
        "ctx",
    )
    return (
        output_full.astype(jnp.bfloat16)[None],
        input_grad[None],
        totals[0],
        totals[1],
        totals[2],
        totals[3],
        totals[4],
        totals[5],
        totals[6],
        totals[7],
        totals[8],
        totals[9],
        totals[10],
        totals[11],
    )


def solution(mesh):
    placed = (
        P("dp", "ctx", None),
        P("dp", "ctx", None),
        P("dp"),
        P("dp"),
        P("dp", None),
        P(None, "dp"),
        P("dp", None),
        P("dp"),
        P("dp"),
        P("dp"),
        P("dp", None),
        P("dp"),
        P("dp", None),
        P("dp"),
    )
    return jax.shard_map(
        per_device,
        mesh=mesh,
        in_specs=placed,
        out_specs=(
            P("dp", "ctx", None),
            P("dp", "ctx", None),
            P("dp"),
            P("dp"),
            P("dp", None),
            P(None, "dp"),
            P("dp", None),
            P("dp"),
            P("dp"),
            P("dp"),
            P("dp", None),
            P("dp"),
            P("dp", None),
            P("dp"),
        ),
        check_vma=False,
    )
```

profile of v0, /device:TPU:0, one launch (start us, length us, event | category | flops | bytes accessed | tf_op | source)
XLA Modules:
  0.0 1175.1 jit_solution(8002505672809796924)
XLA Ops:
  15.9 27.2 %all-reduce.17 = (f32[1088]{0:T(1024)S(1)}, f32[1088]{0:T(1024)S(1)}, f32[1088]{0:T(1024)S(1)}, f32[4352]{0:T(1024)S(1)}, f32[1088]{0:T(1024)S(1)}, /*index=5*/f32[1088]{0:T(1024)S(1)}) all-reduce(f32[1088]{0:T(1024)S(1)} %dynamic-update-slice.1, f32[1088]{0:T(1024)S(1)} %dynamic-update-slice, ...), channel_id=1, replica_groups=mesh['dp'=8,'ctx'=4] {'dp'}, use_global_device_ids=true, to_apply=%add.1 | all-reduce | flops 9792 | bytes 78336
  45.4 17.0 %all-gather.8.cloned.1.call-done = bf16[1088,3264]{1,0:T(8,128)(2,1)} async-done(((bf16[136,3264]{1,0:T(8,128)(2,1)}), bf16[1088,3264]{1,0:T(8,128)(2,1)}) %all-gather.8.cloned.1.call-update) | async-done | bytes 7102480 | tf_op jit(solution)/shard_map/all_gather | solution.py:57
  62.3 6.4 fusion.139
  69.6 8.9 all-gather
  82.8 17.9 %all-gather.10.cloned.1.call-done = bf16[512,1088]{0,1:T(8,128)(2,1)} async-done(((bf16[128,1088]{0,1:T(8,128)(2,1)}), bf16[512,1088]{0,1:T(8,128)(2,1)}) %all-gather.10.cloned.1.call-update) | async-done | bytes 1114128 | tf_op jit(solution)/shard_map/all_gather | solution.py:154
  100.7 2.9 copy.41
  103.5 28.5 %all-gather.12.cloned.1.call-done = bf16[512,1088]{0,1:T(8,128)(2,1)} async-done(((bf16[128,1088]{0,1:T(8,128)(2,1)}), bf16[512,1088]{0,1:T(8,128)(2,1)}) %all-gather.12.cloned.1.call-update) | async-done | bytes 1114128 | tf_op jit(solution)/shard_map/all_gather | solution.py:155
  132.0 3.6 copy.42
  135.6 42.4 %while.37 = (s32[]{:T(128)}, bf16[17,128,64]{1,2,0:T(8,128)(2,1)S(1)}, f32[17,128]{1,0:T(8,128)S(1)}, bf16[17,128,64]{2,1,0:T(8,128)(2,1)}, bf16[17,512,64]{2,1,...) while((s32[]{:T(128)}, ...), condition=%wide.region_5.6_spmd.clone, body=%wide.region_2.5_spmd.clone.sunk | while | flops 17571840 | bytes 1106541 | solution.py:102
  179.6 2.9 fusion.144
  182.6 39.6 %all-gather.16.cloned.1.call-done = bf16[1088,4352]{1,0:T(8,128)(2,1)} async-done(((bf16[136,4352]{1,0:T(8,128)(2,1)}), bf16[1088,4352]{1,0:T(8,128)(2,1)}) %all-gather.16.cloned.1.call-update) | async-done | bytes 9469968 | tf_op jit(solution)/shard_map/all_gather | solution.py:57
  222.2 5.5 convolution_add_fusion
  227.7 57.5 %all-gather.18.cloned.1.call-done = bf16[4352,1088]{1,0:T(8,128)(2,1)} async-done(((bf16[544,1088]{1,0:T(8,128)(2,1)}), bf16[4352,1088]{1,0:T(8,128)(2,1)}) %all-gather.18.cloned.1.call-update) | async-done | bytes 9469968 | tf_op jit(solution)/shard_map/all_gather | solution.py:57
  285.2 6.8 fusion.145
  292.0 2.8 multiply_reduce_fusion.1
  298.9 79.8 %while.39 = (s32[]{:T(128)}, f32[17,512,64]{1,2,0:T(8,128)}, f32[17,512,64]{1,2,0:T(8,128)}, bf16[17,128,64]{2,1,0:T(8,128)(2,1)}, bf16[17,512,64]{2,1,0:T(8,128...) while((s32[]{:T(128)}, f32[17,512,64]{1,2,0:T(8,128)}, ...), condition=%wide.region_14.15_spmd.clone, body=%wide.region_13.14_spmd.clone.sunk | while | flops 34177152 | bytes 1450109 | solution.py:221
  300.1 1.9 fusion.204
  304.8 1.9 fusion.204
  309.5 1.9 fusion.204
  314.2 1.9 fusion.204
  318.9 1.9 fusion.204
  323.6 1.9 fusion.204
  328.2 1.9 fusion.204
  332.9 1.9 fusion.204
  337.6 1.9 fusion.204
  347.0 1.9 fusion.204
  356.4 1.9 fusion.204
  365.8 1.9 fusion.204
  375.2 1.9 fusion.204
  378.7 4.8 pad_maximum_fusion
  384.5 4.1 fusion.133
  388.7 9.7 fusion.123
  399.3 8.4 fusion.130
  407.8 53.2 %while.38 = (s32[]{:T(128)}, f32[17,128,64]{1,2,0:T(8,128)}, bf16[17,128,64]{2,1,0:T(8,128)(2,1)}, bf16[17,512,64]{2,1,0:T(8,128)(2,1)}, f32[17,128]{1,0:T(8,128...) while((s32[]{:T(128)}, f32[17,128,64]{1,2,0:T(8,128)}, ...), condition=%wide.region_12.13_spmd.clone, body=%wide.region_11.12_spmd.clone.sunk | while | flops 25698432 | bytes 1023093 | solution.py:198
  409.0 1.9 fusion.194
  412.2 1.9 fusion.194
  415.3 1.9 fusion.194
  418.4 1.9 fusion.194
  421.5 1.9 fusion.194
  424.7 1.9 fusion.194
  427.8 2.0 fusion.194
  430.9 2.0 fusion.194
  434.1 2.0 fusion.194
  437.2 1.9 fusion.194
  440.3 1.9 fusion.194
  443.4 1.9 fusion.194
  446.5 2.0 fusion.194
  449.7 1.9 fusion.194
  452.8 2.0 fusion.194
  456.0 2.0 fusion.194
  459.1 1.9 fusion.194
  462.1 2.6 reduce-scatter.9.cloned.1.call-done
  466.9 7.4 fusion.127
  474.4 49.1 %reduce-scatter.17.cloned.1.call-done = f32[136,1088]{1,0:T(8,128)} async-done(((f32[1088,1088]{1,0:T(8,128)}), f32[136,1088]{1,0:T(8,128)}) %reduce-scatter.17.cloned.1.call-update) | async-done | bytes 591888
  523.5 135.1 %reduce-scatter.13.cloned.1.call-done = f32[136,4352]{1,0:T(8,128)} async-done(((f32[1088,4352]{1,0:T(8,128)}), f32[136,4352]{1,0:T(8,128)}) %reduce-scatter.13.cloned.1.call-update) | async-done | bytes 2367504 | tf_op jit(solution)/shard_map/reduce_scatter | solution.py:70
  658.6 135.4 %reduce-scatter.15.cloned.1.call-done = f32[544,1088]{1,0:T(8,128)} async-done(((f32[4352,1088]{1,0:T(8,128)}), f32[544,1088]{1,0:T(8,128)}) %reduce-scatter.15.cloned.1.call-update) | async-done | bytes 2367504 | tf_op jit(solution)/shard_map/reduce_scatter | solution.py:70
  793.9 107.3 %reduce-scatter.11.cloned.1.call-done = f32[136,3264]{1,0:T(8,128)} async-done(((f32[1088,3264]{1,0:T(8,128)}), f32[136,3264]{1,0:T(8,128)}) %reduce-scatter.11.cloned.1.call-update) | async-done | bytes 1775632 | tf_op jit(solution)/shard_map/reduce_scatter | solution.py:70
  905.5 6.0 fusion.119
  911.4 25.5 %all-reduce.16 = (f32[1088]{0:T(1024)S(1)}, f32[1088]{0:T(1024)S(1)}, f32[1088]{0:T(1024)S(1)}, f32[2,1088]{1,0:T(2,128)S(1)}, f32[1088]{0:T(1024)S(1)}, /*index...) all-reduce(f32[1088]{0:T(1024)S(1)} %dynamic-update-slice.6, ...), channel_id=1, replica_groups=mesh['dp'=8,'ctx'=4] {'dp'}, use_global_device_ids=true, to_apply=%add.6 | all-reduce | flops 14144 | bytes 113152
  937.5 20.5 %all-reduce.18 = (f32[136]{0:T(256)}, f32[136]{0:T(256)}, f32[2,136]{1,0:T(2,128)}, f32[136]{0:T(256)}, f32[136]{0:T(256)}, /*index=5*/f32[136]{0:T(256)}, f32[544]{0:T(1024)}, f32[136]{0:T(256)}) all-reduce(f32[136]{0:T(256)S(1)} %dynamic-slice.8, f32[136]{0:T(256)S(1)} %dynamic-slice.10, ...), channel_id=1, replica_groups=mesh['dp'=8,'ctx'=4] {'ctx'}, use_global_device_ids=true, to_apply=%region_20.21 | all-reduce | flops 1632 | bytes 13056 | tf_op jit(solution)/shard_map/psum | solution.py:263
  958.0 2.2 fusion.129
  960.2 7.8 fusion.100
  968.0 192.4 %all-reduce.22.cloned.1.call-done = (f32[136,3264]{1,0:T(8,128)}, f32[136,1088]{1,0:T(8,128)}, f32[136,4352]{1,0:T(8,128)}, f32[544,1088]{1,0:T(8,128)}) async-done(((f32[136,3264]{1,0:T(8,128)}, f32[136,1088]{1,0:T(8,128)}, f32[136,4352]{1,0:T(8,128)}, f32[544,1088]{1,0:T(8,128)}), (f32[136,3264]{1,0:T(8,128)}, f32[136,1088]{1,0:T(8,128)}, f32[136,4352]{1,0:T(8,128)}, ...) | async-done | bytes 7102480 | tf_op jit(solution)/shard_map/psum | solution.py:263
  1160.5 3.0 copy.88
  (341 shorter events, 150.6 us)
Async XLA Ops:
  7.2 55.2 %all-gather.8.cloned.1.call-start = ((), (), s32[]{:S(2)}) async-start(), calls=%async_computation.5 | async-start | bytes 8146944 | tf_op jit(solution)/shard_map/all_gather | solution.py:57
  7.9 92.7 %all-gather.10.cloned.1.call-start = ((), (), s32[]{:S(2)}) async-start(), calls=%async_computation.6 | async-start | bytes 1392640 | tf_op jit(solution)/shard_map/all_gather | solution.py:154
  62.3 7.3 copy-start.14
  69.6 62.5 %all-gather.12.cloned.1.call-start = ((), (), s32[]{:S(2)}) async-start(), calls=%async_computation.7 | async-start | bytes 1392640 | tf_op jit(solution)/shard_map/all_gather | solution.py:155
  79.7 99.7 %all-gather.14.cloned.1.call-start = ((), (), s32[]{:S(2)}) async-start(), calls=%async_computation.8 | async-start | bytes 2820096 | tf_op jit(solution)/shard_map/all_gather | solution.py:57
  80.3 142.0 %all-gather.16.cloned.1.call-start = ((), (), s32[]{:S(2)}) async-start(), calls=%async_computation.9 | async-start | bytes 10653696 | tf_op jit(solution)/shard_map/all_gather | solution.py:57
  80.9 204.3 %all-gather.18.cloned.1.call-start = ((), (), s32[]{:S(2)}) async-start(), calls=%async_computation.10 | async-start | bytes 11280384 | tf_op jit(solution)/shard_map/all_gather | solution.py:57
  81.4 383.3 %reduce-scatter.9.cloned.1.call-start = ((), (), s32[]{:S(2)}) async-start(), calls=%async_computation.11 | async-start | bytes 5570560 | tf_op jit(solution)/shard_map/reduce_scatter | solution.py:224
  135.6 44.0 %copy-start.2 = (bf16[1,128,1088]{1,2,0:T(8,128)(2,1)S(1)}, bf16[1,128,1088]{1,2,0:T(8,128)(2,1)}, u32[]{:S(2)}) copy-start(bf16[1,128,1088]{1,2,0:T(8,128)(2,1)} %param.20) | copy-start | bytes 835588
  178.1 1.5 copy-start.5
  178.1 4.4 copy-start.7
  222.2 63.0 %copy-start.11 = (bf16[1,128,1088]{1,2,0:T(8,128)(2,1)S(1)}, bf16[1,128,1088]{1,2,0:T(8,128)(2,1)}, u32[]{:S(2)}) copy-start(bf16[1,128,1088]{1,2,0:T(8,128)(2,1)} %param.21) | copy-start | bytes 835588
  285.2 6.8 copy-start
  292.0 2.8 copy-start.4
  292.0 3.3 copy-start.1
  295.4 0.8 copy-start.3
  383.6 1.0 copy-start.8
  383.6 139.9 %reduce-scatter.17.cloned.1.call-start = ((), (), s32[]{:S(2)}) async-start(), calls=%async_computation.15 | async-start | bytes 5640192
  388.6 269.9 %reduce-scatter.13.cloned.1.call-start = ((), (), s32[]{:S(2)}) async-start(), calls=%async_computation.13 | async-start | bytes 21307392 | tf_op jit(solution)/shard_map/reduce_scatter | solution.py:70
  398.4 1.0 copy-start.12
  398.4 395.5 %reduce-scatter.15.cloned.1.call-start = ((), (), s32[]{:S(2)}) async-start(), calls=%async_computation.14 | async-start | bytes 22560768 | tf_op jit(solution)/shard_map/reduce_scatter | solution.py:70
  407.8 493.4 %reduce-scatter.11.cloned.1.call-start = ((), (), s32[]{:S(2)}) async-start(), calls=%async_computation.12 | async-start | bytes 16293888 | tf_op jit(solution)/shard_map/reduce_scatter | solution.py:70
  466.1 0.8 copy-start.10
  474.3 686.1 %all-reduce.22.cloned.1.call-start = ((), (), s32[]{:S(2)}) async-start(), calls=%async_computation.16 | async-start | bytes 14622720 | tf_op jit(solution)/shard_map/psum | solution.py:263
  901.2 1.3 copy-start.15
  1160.5 3.0 copy-start.13
  1160.5 3.8 copy-start.9
  1164.3 2.6 copy-start.6
Sparse Core Ops, SparseCore 0:
  9.9 52.4 all-gather.7
  69.7 30.9 all-gather.9
  102.8 29.1 all-gather.11
  133.8 27.9 all-gather.13
  163.5 58.6 all-gather.15
  224.0 61.1 all-gather.17
  383.7 81.0 reduce-scatter.8
  468.3 55.2 reduce-scatter.16
  527.1 131.3 reduce-scatter.12
  662.1 131.7 reduce-scatter.14
  797.6 103.5 reduce-scatter.10
  903.7 256.7 all-reduce.21
where the time goes:
time: 1180 us
  waiting for transfers between devices  785 us (67%)
  matrix products  239 us (20%)
  blocking collectives  82.1 us (7%)
  local copies, waits for them, and re-layouts  29.6 us (3%)
  other arithmetic  21.4 us (2%)
  between operations  17.1 us (1%)
    reduce_scatter x3, waiting for transfers between devices, weight_grad(): lax.psum_scatter(lax.dot_general(inputs, grads_low, (((0,), (0,)), ((), (...  378 us
    psum x1, waiting for transfers between devices, per_device(): lax.psum((gain_one_part, shift_one_part, qkv_terms, pair_part, out_terms,...  192 us
    all_gather x4, waiting for transfers between devices, project(): return add_product(inputs, lax.all_gather(weight, 'dp', axis=0, tiled=True))  114 us
    dot_general x51, matrix products, head_scores(): lax.dot_general(query_head, key_head, (((1,), (1,)), ((), ())), preferred...  57 us
    unnamed x2, blocking collectives  52.7 us
    unnamed x13, waiting for transfers between devices  51.5 us
    dot_general x17, matrix products, query_head_grad(): jnp.dot(dscores, key_head, preferred_element_type=jnp.float32) * scale  33.2 us
    dot_general x17, matrix products, key_head_grad(): lax.dot_general(dscores, query_head, (((0,), (0,)), ((), ())), preferred_...  32.4 us
  transfers between devices with their start and end apart: 12, of which 11 were waited for; matrix products, arithmetic and copies ran while one was open for 15% of the time, Pallas kernels for 0%

commit v1 on v0

v1 whole, which is shorter than its diff:
```python
import jax
import jax.numpy as jnp
from jax import lax
from jax.experimental import pallas as pl
from jax.experimental.pallas import tpu as pltpu
from jax.sharding import PartitionSpec as P

D = 1088
H = 17
HD = 64
EVEN = H // 2 * 2 * HD


EPSILON = 1e-05
ROOT_HALF = 0.7071067811865476
INV_ROOT_TAU = 0.3989422804014327

F32 = jnp.float32
LOW = jnp.bfloat16

def norm_parts(values, norm_gain, norm_shift):
    average = jnp.mean(values, axis=-1, keepdims=True)
    centered = values - average
    inverse = lax.rsqrt(jnp.mean(centered * centered, axis=-1, keepdims=True) + EPSILON)
    normed = centered * inverse
    return (normed, inverse, normed * norm_gain + norm_shift)


def norm_back(grad_out, normed, inverse, norm_gain):
    scaled = grad_out * norm_gain
    return inverse * (
        scaled
        - jnp.mean(scaled, axis=-1, keepdims=True)
        - normed * jnp.mean(scaled * normed, axis=-1, keepdims=True)
    )


def gelu_exact(pre_act):
    return 0.5 * pre_act * (1.0 + lax.erf(pre_act * ROOT_HALF))


def gelu_slope(pre_act):
    return (
        0.5 * (1.0 + lax.erf(pre_act * ROOT_HALF))
        + pre_act * jnp.exp(-0.5 * pre_act * pre_act) * INV_ROOT_TAU
    )


def dot(left, right, left_dim, right_dim):
    return lax.dot_general(
        left, right, (((left_dim,), (right_dim,)), ((), ())), preferred_element_type=F32
    )


def gather(block):
    return lax.all_gather(block, "dp", axis=0, tiled=True)


def allowed_pairs(rows, columns):
    first = lax.axis_index("ctx") * rows
    query_pos = first + lax.broadcasted_iota(jnp.int32, (rows, columns), 0)
    key_pos = lax.broadcasted_iota(jnp.int32, (rows, columns), 1)
    return key_pos <= query_pos


def pack_pairs(keys, values):
    return jnp.concatenate(
        [keys[:, :EVEN], values[:, :EVEN], keys[:, EVEN:], values[:, EVEN:]], axis=1
    )


def unpack_pairs(packed):
    return jnp.concatenate(
        [
            packed[:, :EVEN],
            packed[:, 2 * EVEN : 2 * EVEN + HD],
            packed[:, EVEN : 2 * EVEN],
            packed[:, 2 * EVEN + HD :],
        ],
        axis=1,
    )


def over_heads(one_group):
    def step(pair, carry):
        first = pl.multiple_of(pair * 2 * HD, 2 * HD)
        later = pl.multiple_of(EVEN + pair * 2 * HD, 2 * HD)
        one_group(2 * pair, 2, pl.ds(first, 2 * HD), pl.ds(later, 2 * HD))
        return carry

    lax.fori_loop(0, H // 2, step, 0)
    one_group(H - 1, 1, None, None)


def views(head, count, cols, value_cols):
    if count == 2:
        return cols, cols, value_cols
    return slice(EVEN, D), slice(2 * EVEN, 2 * EVEN + HD), slice(2 * EVEN + HD, 2 * D)


def attend_kernel(q_ref, kv_ref, out_ref, log_ref):
    rows, columns = q_ref.shape[0], kv_ref.shape[0]
    allowed = allowed_pairs(rows, columns)
    scale = float(HD) ** (-0.5)
    lane = lax.broadcasted_iota(jnp.int32, (rows, 128), 1)
    log_ref[...] = jnp.zeros((rows, 128), F32)

    def one_group(head, count, cols, value_cols):
        q_cols, k_cols, v_cols = views(head, count, cols, value_cols)
        queries, keys, values = q_ref[:, q_cols], kv_ref[:, k_cols], kv_ref[:, v_cols]
        mixed = []
        logs = log_ref[...]
        for half in range(count):
            own = slice(half * HD, (half + 1) * HD)
            scores = jnp.where(
                allowed, dot(queries[:, own], keys[:, own], 1, 1) * scale, -1e30
            )
            highest = jnp.max(scores, axis=1, keepdims=True)
            powers = jnp.exp(scores - highest)
            summed = jnp.sum(powers, axis=1, keepdims=True)
            probs_low = (powers * (1.0 / summed)).astype(LOW)
            mixed.append(dot(probs_low, values[:, own], 1, 0).astype(LOW))
            logs = jnp.where(lane == head + half, highest + jnp.log(summed), logs)
        log_ref[...] = logs
        out_ref[:, q_cols] = jnp.concatenate(mixed, axis=1) if count == 2 else mixed[0]

    over_heads(one_group)


def attend_back_kernel(q_ref, kv_ref, out_ref, dout_ref, log_ref, dq_ref, dkv_ref, sum_ref):
    rows, columns = q_ref.shape[0], kv_ref.shape[0]
    allowed = allowed_pairs(rows, columns)
    scale = float(HD) ** (-0.5)
    lane = lax.broadcasted_iota(jnp.int32, (rows, 128), 1)

    def one_group(head, count, cols, value_cols):
        q_cols, k_cols, v_cols = views(head, count, cols, value_cols)
        queries, keys, values = q_ref[:, q_cols], kv_ref[:, k_cols], kv_ref[:, v_cols]
        douts, outs, logs = dout_ref[:, q_cols], out_ref[:, q_cols], log_ref[...]
        grads = []
        for half in range(count):
            own = slice(half * HD, (half + 1) * HD)
            query, key, dout = queries[:, own], keys[:, own], douts[:, own]
            log_total = jnp.sum(jnp.where(lane == head + half, logs, 0.0), axis=1, keepdims=True)
            scores = jnp.where(allowed, dot(query, key, 1, 1) * scale, -1e30)
            probs = jnp.exp(scores - log_total)
            delta = jnp.sum(dout.astype(F32) * outs[:, own].astype(F32), axis=1, keepdims=True)
            dscores = (probs * (dot(dout, values[:, own], 1, 1) - delta)).astype(LOW)
            grads.append(
                (
                    dot(dscores, key, 1, 0) * scale,
                    dot(dscores, query, 0, 0) * scale,
                    dot(probs.astype(LOW), dout, 0, 0),
                )
            )
        dquery, dkey, dvalue = [
            jnp.concatenate(terms, axis=1) if count == 2 else terms[0] for terms in zip(*grads)
        ]
        dq_ref[:, q_cols] = dquery.astype(LOW)
        dkv_ref[:, k_cols] = dkey.astype(LOW)
        dkv_ref[:, v_cols] = dvalue.astype(LOW)
        sum_ref[0:1, q_cols] = jnp.sum(dquery, axis=0, keepdims=True)
        sum_ref[1:2, q_cols] = jnp.sum(dvalue, axis=0, keepdims=True)

    over_heads(one_group)


def attend(queries, key_values):
    rows, columns = queries.shape[0], key_values.shape[0]
    return pl.pallas_call(
        attend_kernel,
        out_shape=(
            jax.ShapeDtypeStruct((rows, D), LOW),
            jax.ShapeDtypeStruct((rows, 128), F32),
        ),
        cost_estimate=pl.CostEstimate(
            flops=4 * rows * columns * D,
            bytes_accessed=4 * rows * D + 4 * columns * D,
            transcendentals=H * rows * columns,
        ),
        name="attend",
    )(queries, key_values)


def attend_back(queries, key_values, attended, dattended, logs):
    rows, columns = queries.shape[0], key_values.shape[0]
    return pl.pallas_call(
        attend_back_kernel,
        out_shape=(
            jax.ShapeDtypeStruct((rows, D), LOW),
            jax.ShapeDtypeStruct((columns, 2 * D), LOW),
            jax.ShapeDtypeStruct((2, D), F32),
        ),
        cost_estimate=pl.CostEstimate(
            flops=10 * rows * columns * D,
            bytes_accessed=10 * rows * D + 8 * columns * D,
            transcendentals=H * rows * columns,
        ),
        name="attend_back",
    )(queries, key_values, attended, dattended, logs)


def per_device(
    tokens,
    cotangent,
    ln1_gain,
    ln1_bias,
    qkv_weight,
    qv_bias,
    out_weight,
    out_bias,
    ln2_gain,
    ln2_bias,
    up_weight,
    up_bias,
    down_weight,
    down_bias,
):
    shards = lax.axis_size("dp")
    part = D // shards
    vectors = jnp.concatenate(
        [
            ln1_gain[None],
            ln1_bias[None],
            qv_bias,
            out_bias[None],
            ln2_gain[None],
            ln2_bias[None],
            down_bias[None],
        ],
        axis=0,
    )
    vectors = lax.all_gather(vectors, "dp", axis=0).transpose(1, 0, 2).reshape(8, D)
    gain_one, shift_one, bias_q, bias_v, bias_out, gain_two, shift_two, bias_down = [
        vectors[row] for row in range(8)
    ]
    qkv_full = gather(qkv_weight)
    out_full = gather(out_weight)
    up_cols = lax.all_to_all(up_weight, "dp", 1, 0, tiled=True)
    cot_low = cotangent[0]
    cot_full = cot_low.astype(F32)
    cot_all = gather(cot_low)
    dactivated = dot(cot_all, down_weight, 1, 1)

    inputs_full = tokens[0].astype(F32)
    normed_one, inverse_one, pre_one = norm_parts(inputs_full, gain_one, shift_one)
    act_one = pre_one.astype(LOW)
    mixed_qkv = dot(act_one, qkv_full, 1, 0)
    queries = (mixed_qkv[:, :D] + bias_q).astype(LOW)
    key_values = pack_pairs(mixed_qkv[:, D : 2 * D], mixed_qkv[:, 2 * D :] + bias_v).astype(LOW)
    key_values = lax.all_gather(key_values, "ctx", axis=0, tiled=True)
    attended, logs = attend(queries, key_values)
    hidden_one = inputs_full + (dot(attended, out_full, 1, 0) + bias_out)
    normed_two, inverse_two, pre_two = norm_parts(hidden_one, gain_two, shift_two)
    act_all = gather(pre_two.astype(LOW))
    pre_up = dot(act_all, up_cols, 1, 0) + up_bias
    activated = gelu_exact(pre_up).astype(LOW)
    dpre = dactivated * gelu_slope(pre_up)
    dpre_low = dpre.astype(LOW)
    dnorm_two = lax.psum_scatter(
        dot(dpre_low, up_cols, 1, 1).astype(LOW), "dp", scatter_dimension=0, tiled=True
    ).astype(F32)
    out_terms = lax.psum_scatter(
        dot(activated, down_weight, 1, 0).astype(LOW), "dp", scatter_dimension=0, tiled=True
    ).astype(F32)
    output_full = hidden_one + (out_terms + bias_down)
    down_part = dot(activated, cot_all, 0, 0).astype(LOW)
    up_part = lax.all_to_all(
        dot(act_all, dpre_low, 0, 0).astype(LOW), "dp", 0, 1, tiled=True
    )
    down_grad, up_grad = lax.psum((down_part, up_part), "ctx")

    dhidden = cot_full + norm_back(dnorm_two, normed_two, inverse_two, gain_two)
    dhidden_low = dhidden.astype(LOW)
    dattended = dot(dhidden_low, out_full, 1, 1).astype(LOW)
    out_part = dot(attended, dhidden_low, 0, 0).astype(LOW)
    dqueries, dkv, pair_sums = attend_back(queries, key_values, attended, dattended, logs)
    dkv = lax.psum_scatter(dkv, "ctx", scatter_dimension=0, tiled=True)
    dqkv = jnp.concatenate([dqueries, unpack_pairs(dkv)], axis=1)
    qkv_part = dot(act_one, dqkv, 0, 0).astype(LOW)
    dnorm_one = dot(dqkv, qkv_full, 1, 1)
    input_grad = (dhidden + norm_back(dnorm_one, normed_one, inverse_one, gain_one)).astype(LOW)
    sums = jnp.stack(
        [
            jnp.sum(dnorm_one * normed_one, axis=0),
            jnp.sum(dnorm_one, axis=0),
            pair_sums[0],
            pair_sums[1],
            jnp.sum(dhidden, axis=0),
            jnp.sum(dnorm_two * normed_two, axis=0),
            jnp.sum(dnorm_two, axis=0),
            jnp.sum(cot_full, axis=0),
        ]
    )
    sums = sums.reshape(8, shards, part).transpose(1, 0, 2).reshape(shards, 8 * part)
    sums = jnp.pad(sums.astype(LOW)[:, None], ((0, 0), (0, 15), (0, D - 8 * part)))
    columns = [qkv_part[:, :D], qkv_part[:, D : 2 * D], qkv_part[:, 2 * D :], out_part]
    packed = [column.reshape(shards, part, D) for column in columns] + [sums]
    height = 4 * part + 16
    packed = jnp.concatenate(packed, axis=1).reshape(shards * height, D)
    packed = lax.psum_scatter(packed, "dp", scatter_dimension=0, tiled=True)
    up_sums = jnp.sum(dpre, axis=0)
    packed, up_grad, down_grad = lax.optimization_barrier((packed, up_grad, down_grad))
    packed, up_bias_grad = lax.psum((packed, up_sums), "ctx")
    qkv_grad = jnp.concatenate(
        [packed[row * part : (row + 1) * part] for row in range(3)], axis=1
    ).astype(F32)
    out_grad = packed[3 * part : 4 * part].astype(F32)
    sums = packed[4 * part, : 8 * part].reshape(8, part).astype(F32)
    return (
        output_full.astype(LOW)[None],
        input_grad[None],
        sums[0],
        sums[1],
        qkv_grad,
        sums[2:4],
        out_grad,
        sums[4],
        sums[5],
        sums[6],
        up_grad.astype(F32),
        up_bias_grad,
        down_grad.astype(F32),
        sums[7],
    )


def solution(mesh):
    placed = (
        P("dp", "ctx", None),
        P("dp", "ctx", None),
        P("dp"),
        P("dp"),
        P("dp", None),
        P(None, "dp"),
        P("dp", None),
        P("dp"),
        P("dp"),
        P("dp"),
        P("dp", None),
        P("dp"),
        P("dp", None),
        P("dp"),
    )
    return jax.shard_map(
        per_device,
        mesh=mesh,
        in_specs=placed,
        out_specs=(
            P("dp", "ctx", None),
            P("dp", "ctx", None),
            P("dp"),
            P("dp"),
            P("dp", None),
            P(None, "dp"),
            P("dp", None),
            P("dp"),
            P("dp"),
            P("dp"),
            P("dp", None),
            P("dp"),
            P("dp", None),
            P("dp"),
        ),
        check_vma=False,
    )
```

time: 1180 us -> 642 us (0.54)
  waiting for transfers between devices: 785 us -> 448 us
  matrix products: 239 us -> 41.5 us
  blocking collectives: 82.1 us -> 48.8 us
  Pallas kernels: 0 us -> 21.9 us
  local copies, waits for them, and re-layouts: 29.6 us -> 47.4 us
    reduce_scatter x4 -> x2, waiting for transfers between devices: 380 us -> 93.6 us  [the longest x1 83.4 us: per_device(): packed = lax.psum_scatter(packed, 'dp', scatter_dimension=0, tiled=True)]
    dot_general x131 -> x12, matrix products: 239 us -> 41.5 us  [dot(): lax.dot_general(left, right, (((left_dim,), (right_dim,)), ((), ())), pre...]
    psum x1 -> x2, waiting for transfers between devices: 192 us -> 123 us  [the longest x1 77.6 us: per_device(): down_grad, up_grad = lax.psum((down_part, up_part), 'ctx')]
    unnamed x2 -> x0, blocking collectives: 52.7 us -> none
    unnamed x13, waiting for transfers between devices: 51.5 us -> 79.9 us
    all_to_all x0 -> x1, blocking collectives: none -> 25.6 us  [per_device(): up_cols = lax.all_to_all(up_weight, 'dp', 1, 0, tiled=True)]
    all_gather x6 -> x5, waiting for transfers between devices: 160 us -> 137 us  [the longest x4 90.4 us: gather(): return lax.all_gather(block, 'dp', axis=0, tiled=True)]
    pallas_call x0 -> x2, Pallas kernels: none -> 21.9 us  [the longest x1 11.2 us: attend_back(): pl.pallas_call(attend_back_kernel, out_shape=(jax.ShapeDtypeStruct((rows,...]
  transfers between devices with their start and end apart: 12 -> 12, of which waited for: 11 -> 12; matrix products, arithmetic and copies ran while one was open for 15% -> 9% of each run, Pallas kernels for 0% -> 2%
where the time goes in v1:
time: 642 us; the launch traced here: 641 us
  waiting for transfers between devices  448 us (70%)
  blocking collectives  48.8 us (8%)
  local copies, waits for them, and re-layouts  47.4 us (7%)
  matrix products  41.5 us (6%)
  Pallas kernels  21.9 us (3%)
  other arithmetic  14.6 us (2%)
  between operations  14.3 us (2%)
    all_gather x4, waiting for transfers between devices, gather(): return lax.all_gather(block, 'dp', axis=0, tiled=True)  90.4 us
    reduce_scatter x1, waiting for transfers between devices, per_device(): packed = lax.psum_scatter(packed, 'dp', scatter_dimension=0, tiled=True)  83.4 us
    unnamed x13, waiting for transfers between devices  79.9 us
    psum x1, waiting for transfers between devices, per_device(): down_grad, up_grad = lax.psum((down_part, up_part), 'ctx')  77.6 us
    all_gather x1, waiting for transfers between devices, per_device(): key_values = lax.all_gather(key_values, 'ctx', axis=0, tiled=True)  46.9 us
    psum x1, waiting for transfers between devices, per_device(): packed, up_bias_grad = lax.psum((packed, up_sums), 'ctx')  45.6 us
    dot_general x12, matrix products, dot(): lax.dot_general(left, right, (((left_dim,), (right_dim,)), ((), ())), pre...  41.5 us
    all_to_all x1, blocking collectives, per_device(): up_cols = lax.all_to_all(up_weight, 'dp', 1, 0, tiled=True)  25.6 us
  transfers between devices with their start and end apart: 12, of which 12 were waited for; matrix products, arithmetic and copies ran while one was open for 9% of the time, Pallas kernels for 2%

profile of v1, /device:TPU:0, one launch (start us, length us, event | category | flops | bytes accessed | tf_op | source)
XLA Modules:
  0.0 641.0 jit_solution(11245879045837213575)
XLA Ops:
  8.0 0.8 concatenate.18
  8.8 10.7 %all-gather = f32[64,136]{1,0:T(8,128)S(1)} all-gather(f32[8,136]{1,0:T(8,128)S(1)} %concatenate.18), channel_id=2, replica_groups=mesh['dp'=8,'ctx'=4] {'dp'}, dimensions={0}, use_global_device_ids=true | all-gather | bytes 39168 | tf_op jit(solution)/shard_map/all_gather | solution.py:233
  20.0 1.1 convert_reduce_fusion
  21.2 1.2 fusion.31
  22.4 39.7 %all-gather.8.cloned.1.call-done = bf16[1088,3264]{1,0:T(8,128)(2,1)} async-done(((bf16[136,3264]{1,0:T(8,128)(2,1)}), bf16[1088,3264]{1,0:T(8,128)(2,1)}) %all-gather.8.cloned.1.call-update) | async-done | bytes 7102480 | tf_op jit(solution)/shard_map/all_gather | solution.py:56
  62.1 4.6 fusion.52
  66.6 0.8 fusion.21
  67.7 0.9 concatenate.19
  69.7 46.9 %all-gather.10.cloned.1.call-done.kv_ref = bf16[512,2176]{1,0:T(8,128)(2,1)} async-done(((bf16[128,2176]{1,0:T(8,128)(2,1)}), bf16[512,2176]{1,0:T(8,128)(2,1)}) %all-gather.10.cloned.1.call-update) | async-done | bytes 2228240 | tf_op jit(solution)/shard_map/all_gather | solution.py:251
  116.7 10.7 %attend.1 = (bf16[128,1088]{1,0:T(8,128)(2,1)}, f32[128,128]{1,0:T(8,128)}) custom-call(bf16[128,1088]{1,0:T(8,128)(2,1)} %get-tuple-element.53.q_ref, bf16[512,2176]{1,0:T(8,128)(2,1)} %all-gather.10.cloned.1.call-done.kv_ref), custom_call_target="tpu_custom_call" | custom-call | flops 285212672 | bytes 2785280 | tf_op jit(solution)/shard_map/attend/pallas_call | solution.py:170
  127.4 19.5 %all-gather.12.cloned.1.call-done = bf16[1088,1088]{1,0:T(8,128)(2,1)} async-done(((bf16[136,1088]{1,0:T(8,128)(2,1)}), bf16[1088,1088]{1,0:T(8,128)(2,1)}) %all-gather.12.cloned.1.call-update) | async-done | bytes 2367504 | tf_op jit(solution)/shard_map/all_gather | solution.py:56
  146.9 3.0 fusion.53
  150.0 1.1 add_convert_fusion.1
  151.8 3.5 all_to_all.28
  155.4 25.6 %all_to_all.38 = bf16[136,8,544]{2,0,1:T(8,128)(2,1)S(1)} all-to-all(bf16[136,8,544]{2,0,1:T(8,128)(2,1)S(1)} %copy.74), channel_id=1, replica_groups=mesh['dp'=8,'ctx'=4] {'dp'}, dimensions={1} | all-to-all | bytes 2367488 | tf_op jit(solution)/shard_map/all_to_all | solution.py:239
  181.1 6.2 all-gather.14.cloned.1.call-done
  187.3 5.2 multiply_convert_fusion
  192.5 25.0 %all-gather.16.cloned.1.call-done = bf16[1,1024,1088]{1,2,0:T(8,128)(2,1)} async-done(((bf16[1,128,1088]{1,2,0:T(8,128)(2,1)}), bf16[1,1024,1088]{1,2,0:T(8,128)(2,1)}) %all-gather.16.cloned.1.call-update) | async-done | bytes 2228240 | tf_op jit(solution)/shard_map/all_gather | solution.py:56
  217.5 4.6 fusion.54
  222.1 1.0 copy-done.16
  223.1 3.3 convolution_convert_fusion.2
  226.3 4.1 copy.89
  230.5 1.2 copy-done.15
  231.7 3.4 convolution_convert_fusion.3
  235.1 4.3 copy.87
  239.8 33.2 %reduce-scatter.15.cloned.1.call-done = bf16[128,1088]{1,0:T(8,128)(2,1)} async-done(((bf16[1024,1088]{1,0:T(8,128)(2,1)}), bf16[128,1088]{1,0:T(8,128)(2,1)}) %reduce-scatter.15.cloned.1.call-update) | async-done | bytes 278544
  273.0 1.1 copy.90
  274.6 44.7 %reduce-scatter.13.cloned.1.call-done = bf16[128,1088]{1,0:T(8,128)(2,1)} async-done(((bf16[1024,1088]{1,0:T(8,128)(2,1)}), bf16[128,1088]{1,0:T(8,128)(2,1)}) %reduce-scatter.13.cloned.1.call-update) | async-done | bytes 278544
  319.3 1.1 copy.88
  320.4 1.1 fusion.46
  321.6 2.5 convolution_convert_fusion.6
  324.1 0.9 copy.75.dout_ref
  325.0 11.2 %attend_back.1 = (bf16[128,1088]{1,0:T(8,128)(2,1)}, bf16[512,2176]{1,0:T(8,128)(2,1)}, f32[2,1088]{1,0:T(2,128)}) custom-call(bf16[128,1088]{1,0:T(8,128)(2,1)} %get-tuple-element.53.q_ref, bf16[512,2176]{1,0:T(8,128)(2,1)} %all-gather.10.cloned.1.call-done.kv_ref, bf16[128,1088]{1,0:T(8,128)(2,1)} %get-tuple-element.22.out_ref, ...), custom_call_target="tpu_custom_call" | custom-call | flops 713031680 | bytes 5849088 | tf_op jit(solution)/shard_map/attend_back/pallas_call | solution.py:187
  336.3 3.6 convolution_convert_fusion.5
  339.8 1.6 copy.84
  341.5 3.6 all-to-all-start.1
  345.4 4.7 convolution_convert_fusion.4
  350.1 14.0 %all-to-all-done.1 = bf16[8,136,544]{2,1,0:T(8,128)(2,1)S(1)} async-done(((bf16[8,136,544]{2,1,0:T(8,128)(2,1)}), bf16[8,136,544]{2,1,0:T(8,128)(2,1)S(1)}, u32[]{:S(2)}, u32[]{:S(2)}) %all-to-all-start.1) | async-done | bytes 1183776 | tf_op jit(solution)/shard_map/all_to_all | solution.py:268
  364.0 1.1 copy-done.6
  365.1 1.5 copy.85
  366.7 2.0 all_to_all.35
  369.1 2.3 convolution_convert_fusion.1
  371.9 10.2 %reduce-scatter.9.cloned.1.call-done = bf16[128,2176]{1,0:T(8,128)(2,1)} async-done(((bf16[512,2176]{1,0:T(8,128)(2,1)}), bf16[128,2176]{1,0:T(8,128)(2,1)}) %reduce-scatter.9.cloned.1.call-update) | async-done | bytes 557072 | tf_op jit(solution)/shard_map/reduce_scatter | solution.py:278
  382.1 0.9 fusion.49
  383.0 1.1 fusion.50
  384.5 2.2 convolution_convert_fusion
  386.8 4.0 fusion.48
  390.8 2.2 fusion.30
  393.4 3.5 constant_dynamic-update-slice_fusion.3
  396.9 1.7 constant_dynamic-update-slice_fusion.2
  398.6 0.9 copy-done.3
  399.5 1.6 constant_dynamic-update-slice_fusion.1
  401.2 1.0 copy-done.5
  402.2 1.7 constant_dynamic-update-slice_fusion
  404.7 77.6 %all-reduce.7.cloned.1.call-done = (bf16[136,4352]{1,0:T(8,128)(2,1)}, bf16[544,1088]{1,0:T(8,128)(2,1)}) async-done(((bf16[136,4352]{1,0:T(8,128)(2,1)}, bf16[544,1088]{1,0:T(8,128)(2,1)}), (bf16[136,4352]{1,0:T(8,128)(2,1)}, bf16[544,1088]{1,0:T(8,128)(2,1)})) %all-reduce.7.cloned.1.call-update) | async-done | bytes 2367504 | tf_op jit(solution)/shard_map/psum | solution.py:271
  482.3 83.4 %reduce-scatter.11.cloned.1.call-done = bf16[560,1088]{1,0:T(8,128)(2,1)} async-done(((bf16[4480,1088]{1,0:T(8,128)(2,1)}), bf16[560,1088]{1,0:T(8,128)(2,1)}) %reduce-scatter.11.cloned.1.call-update) | async-done | bytes 1218576 | tf_op jit(solution)/shard_map/reduce_scatter | solution.py:301
  565.7 12.4 %psum.31 = f32[544]{0:T(1024)} all-reduce(f32[544]{0:T(1024)S(1)} %get-tuple-element.76), channel_id=1, replica_groups=mesh['dp'=8,'ctx'=4] {'ctx'}, use_global_device_ids=true, to_apply=%region_22.23 | all-reduce | flops 544 | bytes 4352 | tf_op jit(solution)/shard_map/psum | solution.py:304
  578.1 0.9 fusion.40
  579.1 1.6 convert_element_type.118
  580.6 1.6 convert_element_type.119
  582.3 45.6 %all-reduce.5.cloned.1.call-done = bf16[560,1088]{1,0:T(8,128)(2,1)} async-done(((bf16[560,1088]{1,0:T(8,128)(2,1)}), bf16[560,1088]{1,0:T(8,128)(2,1)}) %all-reduce.5.cloned.1.call-update) | async-done | bytes 1218576 | tf_op jit(solution)/shard_map/psum | solution.py:304
  630.0 2.2 slice_convert_fusion
  632.2 0.9 concatenate.22
  633.1 1.3 convert_element_type.116
  (98 shorter events, 9.4 us)
Async XLA Ops:
  7.2 210.3 %copy-start = (bf16[544,1088]{1,0:T(8,128)(2,1)S(1)}, bf16[544,1088]{1,0:T(8,128)(2,1)}, u32[]{:S(2)}) copy-start(bf16[544,1088]{1,0:T(8,128)(2,1)} %param.26) | copy-start | bytes 3551236
  7.2 54.9 %all-gather.8.cloned.1.call-start = ((), (), s32[]{:S(2)}) async-start(), calls=%async_computation.6 | async-start | bytes 8146944 | tf_op jit(solution)/shard_map/all_gather | solution.py:56
  7.9 108.7 %all-gather.10.cloned.1.call-start = ((), (), s32[]{:S(2)}) async-start(), calls=%async_computation.7 | async-start | bytes 2785280 | tf_op jit(solution)/shard_map/all_gather | solution.py:251
  67.7 79.2 %copy-start.2 = (bf16[1,128,1088]{1,2,0:T(8,128)(2,1)S(1)}, bf16[1,128,1088]{1,2,0:T(8,128)(2,1)}, u32[]{:S(2)}) copy-start(bf16[1,128,1088]{1,2,0:T(8,128)(2,1)} %param.14) | copy-start | bytes 835588
  68.7 78.2 %all-gather.12.cloned.1.call-start = ((), (), s32[]{:S(2)}) async-start(), calls=%async_computation.8 | async-start | bytes 2820096 | tf_op jit(solution)/shard_map/all_gather | solution.py:56
  69.4 117.8 %all-gather.14.cloned.1.call-start = ((), (), s32[]{:S(2)}) async-start(), calls=%async_computation.9 | async-start | bytes 2506752 | tf_op jit(solution)/shard_map/all_gather | solution.py:56
  151.1 66.4 %all-gather.16.cloned.1.call-start = ((), (), s32[]{:S(2)}) async-start(), calls=%async_computation.13 | async-start | bytes 2506752 | tf_op jit(solution)/shard_map/all_gather | solution.py:56
  151.7 121.3 %reduce-scatter.15.cloned.1.call-start = ((), (), s32[]{:S(2)}) async-start(), calls=%async_computation.15 | async-start | bytes 2654208
  155.2 32.0 %copy-start.14 = (f32[544]{0:T(1024)S(1)}, f32[544]{0:T(1024)}, u32[]{:S(2)}) copy-start(f32[544]{0:T(1024)} %param.25) | copy-start | bytes 6532
  222.1 1.0 copy-start.16
  230.5 1.2 copy-start.15
  230.5 88.8 %reduce-scatter.13.cloned.1.call-start = ((), (), s32[]{:S(2)}) async-start(), calls=%async_computation.14 | async-start | bytes 2654208
  239.4 81.0 %copy-start.8 = (bf16[1,128,1088]{1,2,0:T(8,128)(2,1)S(1)}, bf16[1,128,1088]{1,2,0:T(8,128)(2,1)}, u32[]{:S(2)}) copy-start(bf16[1,128,1088]{1,2,0:T(8,128)(2,1)} %param.15) | copy-start | bytes 835588
  239.4 142.7 %reduce-scatter.9.cloned.1.call-start = ((), (), s32[]{:S(2)}) async-start(), calls=%async_computation.10 | async-start | bytes 2785280 | tf_op jit(solution)/shard_map/reduce_scatter | solution.py:278
  341.5 22.6 %all-to-all-start.1 = ((bf16[8,136,544]{2,1,0:T(8,128)(2,1)}), bf16[8,136,544]{2,1,0:T(8,128)(2,1)S(1)}, u32[]{:S(2)}, u32[]{:S(2)}) async-start(bf16[8,136,544]{2,1,0:T(8,128)(2,1)} %bitcast.23), calls=%async_computation.3 | async-start | bytes 2785280 | tf_op jit(solution)/shard_map/all_to_all | solution.py:268
  345.0 137.3 %all-reduce.7.cloned.1.call-start = ((), (), s32[]{:S(2)}) async-start(), calls=%async_computation.16 | async-start | bytes 4874240 | tf_op jit(solution)/shard_map/psum | solution.py:271
  364.0 1.1 copy-start.6
  366.6 2.4 copy-start.7
  368.7 2.7 copy-start.11
  368.7 3.0 copy-start.13
  368.7 15.4 %copy-start.12 = (bf16[128,1088]{1,0:T(8,128)(2,1)S(1)}, bf16[128,1088]{1,0:T(8,128)(2,1)}, u32[]{:S(2)}) copy-start(bf16[128,1088]{1,0:T(8,128)(2,1)} %get-tuple-element.24) | copy-start | bytes 835588
  368.7 196.9 %reduce-scatter.11.cloned.1.call-start = ((), (), s32[]{:S(2)}) async-start(), calls=%async_computation.11 | async-start | bytes 11612160 | tf_op jit(solution)/shard_map/reduce_scatter | solution.py:301
  384.5 6.3 slice-start
  386.8 4.0 slice-start.1
  393.4 3.5 copy-start.4
  396.9 2.6 copy-start.3
  399.5 2.6 copy-start.5
  404.7 223.2 %all-reduce.5.cloned.1.call-start = ((), (), s32[]{:S(2)}) async-start(), calls=%async_computation.12 | async-start | bytes 2580480 | tf_op jit(solution)/shard_map/psum | solution.py:304
  482.3 96.8 %copy-start.10 = (bf16[136,4352]{1,0:T(8,128)(2,1)S(1)}, bf16[136,4352]{1,0:T(8,128)(2,1)}, u32[]{:S(2)}) copy-start(bf16[136,4352]{1,0:T(8,128)(2,1)} %get-tuple-element.28) | copy-start | bytes 3551236
  578.1 2.5 copy-start.9
  632.2 2.3 copy-start.1
Sparse Core Ops, SparseCore 0:
  9.9 52.1 all-gather.7
  68.8 47.8 all-gather.9
  118.5 28.2 all-gather.11
  151.2 35.9 all-gather.13
  189.0 28.4 all-gather.15
  230.6 42.3 reduce-scatter.14
  276.9 42.3 reduce-scatter.12
  336.4 45.6 reduce-scatter.8
  385.1 97.1 all-reduce.6
  485.7 79.9 reduce-scatter.10
  568.0 59.8 all-reduce.4

commit v2 on v1

v2 whole, which is shorter than its diff:
```python
import functools

import jax
import jax.numpy as jnp
from jax import lax
from jax.experimental import pallas as pl
from jax.experimental.pallas import tpu as pltpu
from jax.sharding import PartitionSpec as P

D = 1088
H = 17
HD = 64


EPSILON = 1e-05
ROOT_HALF = 0.7071067811865476
INV_ROOT_TAU = 0.3989422804014327

F32 = jnp.float32
LOW = jnp.bfloat16

def norm_parts(values, norm_gain, norm_shift):
    average = jnp.mean(values, axis=-1, keepdims=True)
    centered = values - average
    inverse = lax.rsqrt(jnp.mean(centered * centered, axis=-1, keepdims=True) + EPSILON)
    normed = centered * inverse
    return (normed, inverse, normed * norm_gain + norm_shift)


def norm_back(grad_out, normed, inverse, norm_gain):
    scaled = grad_out * norm_gain
    return inverse * (
        scaled
        - jnp.mean(scaled, axis=-1, keepdims=True)
        - normed * jnp.mean(scaled * normed, axis=-1, keepdims=True)
    )


def gelu_exact(pre_act):
    return 0.5 * pre_act * (1.0 + lax.erf(pre_act * ROOT_HALF))


def gelu_slope(pre_act):
    return (
        0.5 * (1.0 + lax.erf(pre_act * ROOT_HALF))
        + pre_act * jnp.exp(-0.5 * pre_act * pre_act) * INV_ROOT_TAU
    )


def dot(left, right, left_dim, right_dim):
    return lax.dot_general(
        left, right, (((left_dim,), (right_dim,)), ((), ())), preferred_element_type=F32
    )


def gather(block):
    return lax.all_gather(block, "dp", axis=0, tiled=True)


def spread(block, axis_name):
    return lax.all_to_all(block, axis_name, 0, 0, tiled=True)


def sum_blocks(partial, shards):
    low = partial.astype(LOW).reshape(shards, partial.shape[0] // shards, partial.shape[1])
    return jnp.sum(spread(low, "dp").astype(F32), axis=0)


def to_heads(arrays, parts, width):
    padded = [jnp.pad(array, ((0, 0), (0, parts * width - D))) for array in arrays]
    blocks = [
        jnp.concatenate([array[:, i * width : (i + 1) * width] for array in padded], axis=1)
        for i in range(parts)
    ]
    received = spread(jnp.stack(blocks), "ctx")
    return received.reshape(-1, len(arrays) * width)


def to_rows(stacked, parts, width):
    received = spread(stacked.reshape(parts, -1, stacked.shape[1]), "ctx")
    return [
        jnp.concatenate(
            [received[i, :, first : first + width] for i in range(parts)], axis=1
        )[:, :D]
        for first in range(0, stacked.shape[1], width)
    ]


def allowed_pairs(first, rows, columns):
    query_pos = first + lax.broadcasted_iota(jnp.int32, (rows, columns), 0)
    return lax.broadcasted_iota(jnp.int32, (rows, columns), 1) <= query_pos


def attend_kernel(width, rows, qkv_ref, out_ref, log_ref):
    length = qkv_ref.shape[0]
    scale = float(HD) ** (-0.5)
    lane = lax.broadcasted_iota(jnp.int32, (rows, 128), 1)

    def step(block, carry):
        first = pl.multiple_of(block * rows, rows)
        own = pl.ds(first, rows)
        allowed = allowed_pairs(first, rows, length)
        logs = jnp.zeros((rows, 128), F32)
        mixed = []
        for head in range(width // HD):
            cols = slice(head * HD, (head + 1) * HD)
            key = qkv_ref[:, width + head * HD : width + (head + 1) * HD]
            value = qkv_ref[:, 2 * width + head * HD : 2 * width + (head + 1) * HD]
            scores = jnp.where(allowed, dot(qkv_ref[own, cols], key, 1, 1) * scale, -1e30)
            highest = jnp.max(scores, axis=1, keepdims=True)
            powers = jnp.exp(scores - highest)
            summed = jnp.sum(powers, axis=1, keepdims=True)
            probs_low = (powers * (1.0 / summed)).astype(LOW)
            mixed.append(dot(probs_low, value, 1, 0).astype(LOW))
            logs = jnp.where(lane == head, highest + jnp.log(summed), logs)
        out_ref[own, :] = jnp.concatenate(mixed, axis=1)
        log_ref[own, :] = logs
        return carry

    lax.fori_loop(0, length // rows, step, 0)


def attend_back_kernel(
    width, rows, qkv_ref, out_ref, dout_ref, log_ref, dqkv_ref, sum_ref, key_acc, value_acc
):
    length = qkv_ref.shape[0]
    scale = float(HD) ** (-0.5)
    key_acc[...] = jnp.zeros_like(key_acc)
    value_acc[...] = jnp.zeros_like(value_acc)
    sum_ref[...] = jnp.zeros_like(sum_ref)

    def step(block, carry):
        first = pl.multiple_of(block * rows, rows)
        own = pl.ds(first, rows)
        allowed = allowed_pairs(first, rows, length)
        for head in range(width // HD):
            cols = slice(head * HD, (head + 1) * HD)
            query = qkv_ref[own, cols]
            key = qkv_ref[:, width + head * HD : width + (head + 1) * HD]
            value = qkv_ref[:, 2 * width + head * HD : 2 * width + (head + 1) * HD]
            dout = dout_ref[own, cols]
            scores = jnp.where(allowed, dot(query, key, 1, 1) * scale, -1e30)
            probs = jnp.exp(scores - log_ref[own, head : head + 1])
            delta = jnp.sum(
                dout.astype(F32) * out_ref[own, cols].astype(F32), axis=1, keepdims=True
            )
            dscores = (probs * (dot(dout, value, 1, 1) - delta)).astype(LOW)
            dquery = dot(dscores, key, 1, 0) * scale
            dqkv_ref[own, cols] = dquery.astype(LOW)
            sum_ref[0:1, cols] += jnp.sum(dquery, axis=0, keepdims=True)
            key_acc[:, cols] += dot(dscores, query, 0, 0) * scale
            value_acc[:, cols] += dot(probs.astype(LOW), dout, 0, 0)
        return carry

    lax.fori_loop(0, length // rows, step, 0)
    dqkv_ref[:, width : 2 * width] = key_acc[...].astype(LOW)
    dqkv_ref[:, 2 * width :] = value_acc[...].astype(LOW)
    sum_ref[1:2, :] = jnp.sum(value_acc[...], axis=0, keepdims=True)


def attend(qkv, width, rows):
    length = qkv.shape[0]
    return pl.pallas_call(
        functools.partial(attend_kernel, width, rows),
        out_shape=(
            jax.ShapeDtypeStruct((length, width), LOW),
            jax.ShapeDtypeStruct((length, 128), F32),
        ),
        cost_estimate=pl.CostEstimate(
            flops=4 * length * length * width,
            bytes_accessed=8 * length * width,
            transcendentals=length * length * width // HD,
        ),
        name="attend",
    )(qkv)


def attend_back(qkv, attended, dattended, logs, width, rows):
    length = qkv.shape[0]
    return pl.pallas_call(
        functools.partial(attend_back_kernel, width, rows),
        out_shape=(
            jax.ShapeDtypeStruct((length, 3 * width), LOW),
            jax.ShapeDtypeStruct((2, width), F32),
        ),
        scratch_shapes=[pltpu.VMEM((length, width), F32), pltpu.VMEM((length, width), F32)],
        cost_estimate=pl.CostEstimate(
            flops=10 * length * length * width,
            bytes_accessed=16 * length * width,
            transcendentals=length * length * width // HD,
        ),
        name="attend_back",
    )(qkv, attended, dattended, logs)


def per_device(
    tokens,
    cotangent,
    ln1_gain,
    ln1_bias,
    qkv_weight,
    qv_bias,
    out_weight,
    out_bias,
    ln2_gain,
    ln2_bias,
    up_weight,
    up_bias,
    down_weight,
    down_bias,
):
    shards = lax.axis_size("dp")
    part = D // shards
    vectors = jnp.concatenate(
        [
            ln1_gain[None],
            ln1_bias[None],
            qv_bias,
            out_bias[None],
            ln2_gain[None],
            ln2_bias[None],
            down_bias[None],
        ],
        axis=0,
    )
    vectors = lax.all_gather(vectors, "dp", axis=0).transpose(1, 0, 2).reshape(8, D)
    gain_one, shift_one, bias_q, bias_v, bias_out, gain_two, shift_two, bias_down = [
        vectors[row] for row in range(8)
    ]
    parts = lax.axis_size("ctx")
    width = -(-H // parts) * HD
    local_count = tokens.shape[1]
    qkv_full = gather(qkv_weight)
    up_cols = lax.all_to_all(up_weight, "dp", 1, 0, tiled=True)
    cot_low = cotangent[0]
    cot_full = cot_low.astype(F32)
    qkv_full, out_low, cot_low = lax.optimization_barrier((qkv_full, out_weight, cot_low))
    out_full = gather(out_low)
    out_full, cot_low = lax.optimization_barrier((out_full, cot_low))
    cot_all = gather(cot_low)
    dactivated = dot(cot_all, down_weight, 1, 1)

    inputs_full = tokens[0].astype(F32)
    normed_one, inverse_one, pre_one = norm_parts(inputs_full, gain_one, shift_one)
    act_one = pre_one.astype(LOW)
    mixed_qkv = dot(act_one, qkv_full, 1, 0)
    head_qkv = to_heads(
        [
            (mixed_qkv[:, :D] + bias_q).astype(LOW),
            mixed_qkv[:, D : 2 * D].astype(LOW),
            (mixed_qkv[:, 2 * D :] + bias_v).astype(LOW),
        ],
        parts,
        width,
    )
    head_out, logs = attend(head_qkv, width, local_count)
    (attended,) = to_rows(head_out, parts, width)
    hidden_one = inputs_full + (dot(attended, out_full, 1, 0) + bias_out)
    normed_two, inverse_two, pre_two = norm_parts(hidden_one, gain_two, shift_two)
    act_two, cot_all, up_cols = lax.optimization_barrier(
        (pre_two.astype(LOW), cot_all, up_cols)
    )
    act_all = gather(act_two)
    act_all, act_one_late = lax.optimization_barrier((act_all, act_one))
    act_one_all = gather(act_one_late)
    pre_up = dot(act_all, up_cols, 1, 0) + up_bias
    activated = gelu_exact(pre_up).astype(LOW)
    dpre = dactivated * gelu_slope(pre_up)
    dpre_low = dpre.astype(LOW)
    dnorm_two = sum_blocks(dot(dpre_low, up_cols, 1, 1), shards)
    dnorm_two, activated = lax.optimization_barrier((dnorm_two, activated))
    down_part = dot(activated, cot_all, 0, 0).astype(LOW)
    up_part = lax.all_to_all(
        dot(act_all, dpre_low, 0, 0).astype(LOW), "dp", 0, 1, tiled=True
    )
    down_grad, up_grad = lax.psum((down_part, up_part), "ctx")

    dhidden = cot_full + norm_back(dnorm_two, normed_two, inverse_two, gain_two)
    dhidden_low = dhidden.astype(LOW)
    dattended = dot(dhidden_low, out_full, 1, 1).astype(LOW)
    out_grad = lax.psum_scatter(
        dot(attended, dhidden_low, 0, 0).astype(LOW), "dp", scatter_dimension=0, tiled=True
    )
    head_dout = to_heads([dattended], parts, width)
    head_dqkv, head_sums = attend_back(head_qkv, head_out, head_dout, logs, width, local_count)
    dqkv = jnp.concatenate(to_rows(head_dqkv, parts, width), axis=1)
    pair_sums = lax.dynamic_update_slice(
        jnp.zeros((2, parts * width), F32), head_sums, (0, lax.axis_index("ctx") * width)
    )[:, :D]
    dqkv_all = lax.all_to_all(dqkv, "dp", 1, 0, tiled=True)
    qkv_part = dot(act_one_all, dqkv_all, 0, 0).astype(LOW)
    dnorm_one = dot(dqkv, qkv_full, 1, 1)
    input_grad = (dhidden + norm_back(dnorm_one, normed_one, inverse_one, gain_one)).astype(LOW)
    sums = jnp.stack(
        [
            jnp.sum(dnorm_one * normed_one, axis=0),
            jnp.sum(dnorm_one, axis=0),
            pair_sums[0],
            pair_sums[1],
            jnp.sum(dhidden, axis=0),
            jnp.sum(dnorm_two * normed_two, axis=0),
            jnp.sum(dnorm_two, axis=0),
            jnp.sum(cot_full, axis=0),
        ]
    )
    sums = sums.reshape(8, shards, part).transpose(1, 0, 2).reshape(shards, 8 * part)
    columns = 3 * part
    sums = jnp.pad(sums.astype(LOW), ((0, 0), (0, part))).reshape(shards, 3, columns)
    spare = -(part + 3) % 16
    packed = jnp.concatenate(
        [qkv_part.reshape(shards, part, columns), jnp.pad(sums, ((0, 0), (0, spare), (0, 0)))],
        axis=1,
    )
    packed = spread(packed, "dp")
    qkv_mine = packed[:, :part].transpose(1, 0, 2).reshape(part, 3 * D)
    sums_mine = jnp.sum(
        packed[:, part : part + 3].astype(F32).reshape(shards, 9 * part)[:, : 8 * part], axis=0
    )
    qkv_mine, activated = lax.optimization_barrier((qkv_mine, activated))
    output_full = hidden_one + (sum_blocks(dot(activated, down_weight, 1, 0), shards) + bias_down)
    small = jnp.concatenate([sums_mine, jnp.sum(dpre, axis=0)])
    qkv_mine, up_grad, down_grad, small, out_grad = lax.optimization_barrier(
        (qkv_mine, up_grad, down_grad, small, out_grad)
    )
    qkv_grad, out_grad, small = lax.psum((qkv_mine, out_grad, small), "ctx")
    qkv_grad = qkv_grad.astype(F32)
    out_grad = out_grad.astype(F32)
    sums = small[: 8 * part].reshape(8, part)
    up_bias_grad = small[8 * part :]
    return (
        output_full.astype(LOW)[None],
        input_grad[None],
        sums[0],
        sums[1],
        qkv_grad,
        sums[2:4],
        out_grad,
        sums[4],
        sums[5],
        sums[6],
        up_grad.astype(F32),
        up_bias_grad,
        down_grad.astype(F32),
        sums[7],
    )


def solution(mesh):
    placed = (
        P("dp", "ctx", None),
        P("dp", "ctx", None),
        P("dp"),
        P("dp"),
        P("dp", None),
        P(None, "dp"),
        P("dp", None),
        P("dp"),
        P("dp"),
        P("dp"),
        P("dp", None),
        P("dp"),
        P("dp", None),
        P("dp"),
    )
    return jax.shard_map(
        per_device,
        mesh=mesh,
        in_specs=placed,
        out_specs=(
            P("dp", "ctx", None),
            P("dp", "ctx", None),
            P("dp"),
            P("dp"),
            P("dp", None),
            P(None, "dp"),
            P("dp", None),
            P("dp"),
            P("dp"),
            P("dp"),
            P("dp", None),
            P("dp"),
            P("dp", None),
            P("dp"),
        ),
        check_vma=False,
    )
```

time: 642 us -> 536 us (0.83); the launches traced: 641 us -> 527 us
  waiting for transfers between devices: 448 us -> 251 us
  blocking collectives: 48.8 us -> 91.1 us
  starting transfers between devices: 4.5 us -> 29.1 us
  other arithmetic: 14.6 us -> 36.4 us
    reduce_scatter x2 -> x0, waiting for transfers between devices: 93.6 us -> none  [the longest x1 83.4 us: per_device(): packed = lax.psum_scatter(packed, 'dp', scatter_dimension=0, tiled=True)]
    all_to_all x0 -> x6, waiting for transfers between devices: none -> 87.3 us  [the longest x4 60.8 us: spread(): return lax.all_to_all(block, axis_name, 0, 0, tiled=True)]
    unnamed x13 -> x8, waiting for transfers between devices: 79.9 us -> 1.31 us
    psum x1, waiting for transfers between devices: 77.6 us -> 0.01 us  [per_device(): down_grad, up_grad = lax.psum((down_part, up_part), 'ctx')]
    all_gather x1 -> x0, waiting for transfers between devices: 46.9 us -> none  [per_device(): key_values = lax.all_gather(key_values, 'ctx', axis=0, tiled=True)]
    all_to_all x1 -> x3, blocking collectives: 25.6 us -> 69.5 us  [spread(): return lax.all_to_all(block, axis_name, 0, 0, tiled=True)]
    all_to_all x0 -> x6, starting transfers between devices: none -> 24.6 us  [the longest x4 16.4 us: spread(): return lax.all_to_all(block, axis_name, 0, 0, tiled=True)]
    unnamed x46 -> x60, local copies, waits for them, and re-layouts: 24.6 us -> 4.54 us
  transfers between devices with their start and end apart: 12 -> 15, of which waited for: 12 -> 11; matrix products, arithmetic and copies ran while one was open for 9% -> 18% of each run, Pallas kernels for 2% -> 4%
where the time goes in v2:
time: 536 us; the launch traced here: 527 us
  waiting for transfers between devices  251 us (47%)
  blocking collectives  91.1 us (17%)
  matrix products  41.5 us (8%)
  local copies, waits for them, and re-layouts  41.4 us (8%)
  other arithmetic  36.4 us (7%)
  starting transfers between devices  29.1 us (5%)
  Pallas kernels  22 us (4%)
  between operations  15.3 us (3%)
    all_gather x5, waiting for transfers between devices, gather(): return lax.all_gather(block, 'dp', axis=0, tiled=True)  91.2 us
    all_to_all x3, blocking collectives, spread(): return lax.all_to_all(block, axis_name, 0, 0, tiled=True)  69.5 us
    all_to_all x4, waiting for transfers between devices, spread(): return lax.all_to_all(block, axis_name, 0, 0, tiled=True)  60.8 us
    dot_general x12, matrix products, dot(): lax.dot_general(left, right, (((left_dim,), (right_dim,)), ((), ())), pre...  41.5 us
    psum x1, waiting for transfers between devices, per_device(): qkv_grad, out_grad, small = lax.psum((qkv_mine, out_grad, small), 'ctx')  36.6 us
    optimization_barrier x1, waiting for transfers between devices, per_device(): lax.optimization_barrier((qkv_mine, up_grad, down_grad, small, out_grad))  18.1 us
    all_to_all x4, starting transfers between devices, spread(): return lax.all_to_all(block, axis_name, 0, 0, tiled=True)  16.4 us
    all_to_all x1, waiting for transfers between devices, per_device(): lax.all_to_all(dot(act_all, dpre_low, 0, 0).astype(LOW), 'dp', 0, 1, tile...  16 us
  transfers between devices with their start and end apart: 15, of which 11 were waited for; matrix products, arithmetic and copies ran while one was open for 18% of the time, Pallas kernels for 4%

profile of v2, /device:TPU:0, one launch (start us, length us, event | category | flops | bytes accessed | tf_op | source)
XLA Modules:
  0.0 527.4 jit_solution(6522210854779214653)
XLA Ops:
  8.0 54.1 %all-gather.7.cloned.1.call-done = bf16[1088,3264]{1,0:T(8,128)(2,1)} async-done(((bf16[136,3264]{1,0:T(8,128)(2,1)}), bf16[1088,3264]{1,0:T(8,128)(2,1)}) %all-gather.7.cloned.1.call-update) | async-done | bytes 7102480 | tf_op jit(solution)/shard_map/all_gather | solution.py:57
  62.9 9.2 %all-gather = f32[64,136]{1,0:T(8,128)S(1)} all-gather(f32[8,136]{1,0:T(8,128)S(1)} %concatenate.38), channel_id=2, replica_groups=mesh['dp'=8,'ctx'=4] {'dp'}, dimensions={0}, use_global_device_ids=true | all-gather | bytes 39168 | tf_op jit(solution)/shard_map/all_gather | solution.py:226
  73.2 1.1 convert_reduce_fusion.2
  74.3 1.1 fusion.34
  75.8 6.1 %fusion.51 = (bf16[128,3264]{0,1:T(8,128)(2,1)S(1)}, f32[128,3264]{0,1:T(8,128)S(1)}) fusion(bf16[128,1088]{0,1:T(8,128)(2,1)S(1)} %fusion.27, bf16[1088,3264]{1,0:T(8,128)(2,1)} %all-gather.7.cloned.1.call-done), kind=kOutput, calls=%fused_computation.149 | convolution fusion | flops 909533184 | bytes 9887744 | tf_op jit(solution)/shard_map/dot_general | solution.py:51
  82.5 11.0 %all-gather.9.cloned.1.call-done = bf16[1088,1088]{1,0:T(8,128)(2,1)} async-done(((bf16[136,1088]{1,0:T(8,128)(2,1)}), bf16[1088,1088]{1,0:T(8,128)(2,1)}) %all-gather.9.cloned.1.call-update) | async-done | bytes 2367504 | tf_op jit(solution)/shard_map/all_gather | solution.py:57
  93.7 29.1 %all_to_all.92 = bf16[4,128,960]{1,2,0:T(8,128)(2,1)S(1)} all-to-all(bf16[4,128,960]{1,2,0:T(8,128)(2,1)S(1)} %pad_maximum_fusion), channel_id=1, replica_groups=mesh['dp'=8,'ctx'=4] {'ctx'}, dimensions={0} | all-to-all | bytes 1966080 | tf_op jit(solution)/shard_map/all_to_all | solution.py:61
  122.8 1.3 copy.49
  124.1 10.1 %attend.1 = (bf16[512,320]{1,0:T(8,128)(2,1)}, f32[512,128]{1,0:T(8,128)}) custom-call(bf16[512,960]{1,0:T(8,128)(2,1)} %bitcast.161), custom_call_target="tpu_custom_call" | custom-call | flops 335544320 | bytes 1310720 | tf_op jit(solution)/shard_map/attend/pallas_call | solution.py:163
  134.2 1.9 copy.50
  136.1 3.5 all-to-all-start.1
  139.8 3.5 all_to_all.65
  143.3 1.3 copy.51
  144.5 4.7 all-to-all-done.1
  149.2 3.6 all-to-all-start.2
  153.7 2.9 fusion.52
  156.8 1.1 add_convert_fusion.1
  157.8 14.0 %all-to-all-done.2 = bf16[136,8,544]{2,0,1:T(8,128)(2,1)S(1)} async-done(((bf16[136,8,544]{2,0,1:T(8,128)(2,1)}), bf16[136,8,544]{2,0,1:T(8,128)(2,1)S(1)}, u32[]{:S(2)}, u32[]{:S(2)}) %all-to-all-start.2) | async-done | bytes 1183776 | tf_op jit(solution)/shard_map/all_to_all | solution.py:234
  171.8 26.1 %all-gather.13.cloned.1.call-done = bf16[1024,1088]{0,1:T(8,128)(2,1)} async-done(((bf16[128,1088]{0,1:T(8,128)(2,1)}), bf16[1024,1088]{0,1:T(8,128)(2,1)}) %all-gather.13.cloned.1.call-update) | async-done | bytes 2228240 | tf_op jit(solution)/shard_map/all_gather | solution.py:57
  197.9 4.7 multiply_convert_fusion
  202.6 3.2 fusion.53
  205.8 1.0 copy-done.26
  206.8 1.6 convolution_convert_fusion.4
  208.5 1.6 copy.60
  210.1 3.6 all-to-all-start.9
  214.3 3.6 fusion.11
  217.8 1.8 copy.72
  219.6 16.0 %all-to-all-done.9 = bf16[8,136,544]{2,1,0:T(8,128)(2,1)S(1)} async-done(((bf16[8,136,544]{2,1,0:T(8,128)(2,1)}), bf16[8,136,544]{2,1,0:T(8,128)(2,1)S(1)}, u32[]{:S(2)}, u32[]{:S(2)}) %all-to-all-start.9) | async-done | bytes 1183776 | tf_op jit(solution)/shard_map/all_to_all | solution.py:273
  235.7 1.1 copy-done.2
  236.7 4.4 all-to-all-start.3
  241.4 1.5 copy.61
  242.9 2.0 all_to_all.81
  244.9 28.0 %all-to-all-done.3 = bf16[8,128,1088]{1,2,0:T(8,128)(2,1)} async-done(((bf16[8,128,1088]{1,2,0:T(8,128)(2,1)}), bf16[8,128,1088]{1,2,0:T(8,128)(2,1)}, u32[]{:S(2)}, u32[]{:S(2)}) %all-to-all-start.3) | async-done | bytes 2228256 | tf_op jit(solution)/shard_map/all_to_all | solution.py:61
  272.9 2.0 convert_reduce_fusion.1
  278.5 2.7 convolution_convert_fusion.3
  281.3 20.9 %all_to_all.93 = bf16[4,128,320]{1,2,0:T(8,128)(2,1)} all-to-all(bf16[4,128,320]{1,2,0:T(8,128)(2,1)S(1)} %pad_maximum_fusion.8), channel_id=1, replica_groups=mesh['dp'=8,'ctx'=4] {'ctx'}, dimensions={0} | all-to-all | bytes 655360 | tf_op jit(solution)/shard_map/all_to_all | solution.py:61
  302.2 1.9 copy.53
  304.1 12.0 %attend_back.1 = (bf16[512,960]{1,0:T(8,128)(2,1)}, f32[2,320]{1,0:T(2,128)}) custom-call(bf16[512,960]{1,0:T(8,128)(2,1)} %bitcast.162, bf16[512,320]{1,0:T(8,128)(2,1)} %get-tuple-element.38.out_ref, bf16[512,320]{1,0:T(8,128)(2,1)} %bitcast.165, f32[512,128]{1,0:T(8,128)} %get-tuple-element.48.log_ref), custom_call_target="tpu_custom_call" | custom-call | flops 838860800 | bytes 2621440 | tf_op jit(solution)/shard_map/attend_back/pallas_call | solution.py:180
  316.1 2.3 copy.54
  318.4 4.2 all-to-all-start.5
  323.6 2.3 convolution_convert_fusion
  326.2 28.1 %all-to-all-done.5 = bf16[4,128,960]{1,2,0:T(8,128)(2,1)} async-done(((bf16[4,128,960]{1,2,0:T(8,128)(2,1)}), bf16[4,128,960]{1,2,0:T(8,128)(2,1)}, u32[]{:S(2)}, u32[]{:S(2)}) %all-to-all-start.5) | async-done | bytes 983072 | tf_op jit(solution)/shard_map/all_to_all | solution.py:61
  354.3 1.3 slice_bitcast_fusion.12
  355.7 13.6 %fusion.15 = bf16[128,3264]{0,1:T(8,128)(2,1)} fusion(bf16[128,320]{0,1:T(8,128)(2,1)S(1)} %get-tuple-element.85, bf16[128,320]{0,1:T(8,128)(2,1)S(1)} %get-tuple-element.86, bf16[128,320]{0,1:T(8,128)(2,1)S(1)} %get-tuple-element.87, bf16[128,320]{0,1:T(8,128)(2,1)S(1)} %get-tuple-element.88, bf16[128,320]{0,1:T(8,128)(2,1)S(1)} %get-tuple-element.89, ...), kind=kLoop, calls=%fused_computation.36 | loop fusion | flops 12533760 | bytes 1818624 | tf_op jit(solution)/shard_map/concatenate | solution.py:286
  369.3 6.6 %fusion.29 = (f32[128]{0:T(128)}, bf16[1088]{0:T(1024)(128)(2,1)S(1)}, f32[128]{0:T(128)}, bf16[1088]{0:T(1024)(128)(2,1)S(1)}, f32[128,1088]{0,1:T(8,128)}) fusion(bf16[1,128,1088]{1,2,0:T(8,128)(2,1)S(1)} %copy-done.3, f32[1088]{0:T(1024)S(1)} %mul.134, f32[128]{0:T(128)S(1)} %add_rsqrt_fusion.1, f32[128]{0:T(128)S(1)} %broadcast_multiply_fusion.5, ...), kind=kOutput, calls=%fused_computation.59 | convolution fusion | flops 910505600 | bytes 8784384 | tf_op jit(solution)/shard_map/dot_general | solution.py:51
  375.9 4.6 all-to-all-start.6
  381.0 12.6 %all-to-all-done.6 = bf16[128,8,408]{0,2,1:T(8,128)(2,1)S(1)} async-done(((bf16[128,8,408]{0,2,1:T(8,128)(2,1)}), bf16[128,8,408]{0,2,1:T(8,128)(2,1)S(1)}, u32[]{:S(2)}, u32[]{:S(2)}) %all-to-all-start.6) | async-done | bytes 835616 | tf_op jit(solution)/shard_map/all_to_all | solution.py:290
  393.6 3.9 convolution_convert_fusion.5
  397.4 1.8 copy.56
  399.5 19.4 %all_to_all.94 = bf16[8,144,408]{2,1,0:T(8,128)(2,1)S(1)} all-to-all(bf16[8,144,408]{2,1,0:T(8,128)(2,1)S(1)} %fusion.12), channel_id=1, replica_groups=mesh['dp'=8,'ctx'=4] {'dp'}, dimensions={0} | all-to-all | bytes 1880064 | tf_op jit(solution)/shard_map/all_to_all | solution.py:61
  419.0 1.3 copy.58
  420.3 3.3 reshape.180
  423.6 3.2 fusion.10
  426.8 1.8 copy.71
  428.5 4.4 all-to-all-start.8
  433.0 1.4 add.154
  436.6 18.1 %reduce-scatter.4.cloned.1.call-done = bf16[136,1088]{1,0:T(8,128)(2,1)} async-done(((bf16[1088,1088]{1,0:T(8,128)(2,1)}), bf16[136,1088]{1,0:T(8,128)(2,1)}) %reduce-scatter.4.cloned.1.call-update) | async-done | bytes 295952 | tf_op jit(solution)/shard_map/optimization_barrier | solution.py:322
  456.0 2.1 fusion.40
  458.1 12.4 %psum.37 = f32[1632]{0:T(1024)S(1)} all-reduce(f32[1632]{0:T(1024)S(1)} %pad_maximum_fusion.14), channel_id=1, replica_groups=mesh['dp'=8,'ctx'=4] {'ctx'}, use_global_device_ids=true, to_apply=%region_21.22 | all-reduce | flops 1632 | bytes 13056 | tf_op jit(solution)/shard_map/psum | solution.py:325
  471.3 2.9 convert_element_type.119
  474.2 1.6 convert_element_type.118
  477.1 36.6 %all-reduce.12.cloned.1.call-done = (bf16[136,3264]{1,0:T(8,128)(2,1)}, bf16[136,1088]{1,0:T(8,128)(2,1)}) async-done(((bf16[136,3264]{1,0:T(8,128)(2,1)}, bf16[136,1088]{1,0:T(8,128)(2,1)}), (bf16[136,3264]{1,0:T(8,128)(2,1)}, bf16[136,1088]{1,0:T(8,128)(2,1)})) %all-reduce.12.cloned.1.call-update) | async-done | bytes 1183760 | tf_op jit(solution)/shard_map/psum | solution.py:325
  513.7 2.6 convert_element_type.116
  517.1 2.0 convert_reduce_fusion
  (141 shorter events, 18.8 us)
Async XLA Ops:
  7.2 195.4 %copy-start = (bf16[544,1088]{1,0:T(8,128)(2,1)S(1)}, bf16[544,1088]{1,0:T(8,128)(2,1)}, u32[]{:S(2)}) copy-start(bf16[544,1088]{1,0:T(8,128)(2,1)} %param.26) | copy-start | bytes 3551236
  7.2 68.2 %copy-start.3 = (bf16[1,128,1088]{1,2,0:T(8,128)(2,1)S(1)}, bf16[1,128,1088]{1,2,0:T(8,128)(2,1)}, u32[]{:S(2)}) copy-start(bf16[1,128,1088]{1,2,0:T(8,128)(2,1)} %param.14) | copy-start | bytes 835588
  7.2 54.9 %all-gather.7.cloned.1.call-start = ((), (), s32[]{:S(2)}) async-start(), calls=%async_computation.11 | async-start | bytes 8146944 | tf_op jit(solution)/shard_map/all_gather | solution.py:57
  7.9 85.5 %all-gather.9.cloned.1.call-start = ((), (), s32[]{:S(2)}) async-start(), calls=%async_computation.12 | async-start | bytes 2820096 | tf_op jit(solution)/shard_map/all_gather | solution.py:57
  62.1 109.7 %all-gather.11.cloned.1.call-start = ((), (), s32[]{:S(2)}) async-start(), calls=%async_computation.13 | async-start | bytes 2506752 | tf_op jit(solution)/shard_map/all_gather | solution.py:57
  74.3 295.0 %copy-start.18 = (f32[128]{0:T(128)}, f32[128]{0:T(128)S(1)}, u32[]{:S(2)}) copy-start(f32[128]{0:T(128)S(1)} %broadcast_multiply_fusion.5) | copy-start | bytes 1540
  75.4 293.9 %copy-start.20 = (f32[128]{0:T(128)}, f32[128]{0:T(128)S(1)}, u32[]{:S(2)}) copy-start(f32[128]{0:T(128)S(1)} %add_rsqrt_fusion.1) | copy-start | bytes 1540
  75.8 6.1 %copy-start.4 = (bf16[128,1088]{0,1:T(8,128)(2,1)}, bf16[128,1088]{0,1:T(8,128)(2,1)S(1)}, u32[]{:S(2)}) copy-start(bf16[128,1088]{0,1:T(8,128)(2,1)S(1)} %fusion.27) | copy-start | bytes 835588
  136.1 13.2 %all-to-all-start.1 = ((bf16[4,128,320]{1,2,0:T(8,128)(2,1)}), bf16[4,128,320]{1,2,0:T(8,128)(2,1)S(1)}, u32[]{:S(2)}, u32[]{:S(2)}) async-start(bf16[4,128,320]{1,2,0:T(8,128)(2,1)} %copy.50), calls=%async_computation.1 | async-start | bytes 655360 | tf_op jit(solution)/shard_map/all_to_all | solution.py:61
  149.2 22.6 %all-to-all-start.2 = ((bf16[136,8,544]{2,0,1:T(8,128)(2,1)}), bf16[136,8,544]{2,0,1:T(8,128)(2,1)S(1)}, u32[]{:S(2)}, u32[]{:S(2)}) async-start(bf16[136,8,544]{2,0,1:T(8,128)(2,1)} %copy.51), calls=%async_computation.2 | async-start | bytes 2785280 | tf_op jit(solution)/shard_map/all_to_all | solution.py:234
  152.8 45.1 %all-gather.13.cloned.1.call-start = ((), (), s32[]{:S(2)}) async-start(), calls=%async_computation.14 | async-start | bytes 2506752 | tf_op jit(solution)/shard_map/all_gather | solution.py:57
  153.0 0.6 copy-start.8
  153.1 3.5 copy-start.10
  153.1 3.5 copy-start.12
  153.1 3.5 copy-start.14
  153.7 44.2 %copy-start.24 = (f32[544]{0:T(1024)S(1)}, f32[544]{0:T(1024)}, u32[]{:S(2)}) copy-start(f32[544]{0:T(1024)} %param.25) | copy-start | bytes 6532
  171.8 30.8 %copy-start.6 = (bf16[136,8,544]{2,0,1:T(8,128)(2,1)}, bf16[136,8,544]{2,0,1:T(8,128)(2,1)S(1)}, u32[]{:S(2)}) copy-start(bf16[136,8,544]{2,0,1:T(8,128)(2,1)S(1)} %all-to-all-done.2) | copy-start | bytes 3551236
  197.9 4.7 copy-start.21
  202.6 4.2 copy-start.23
  205.8 1.0 copy-start.26
  210.1 25.6 %all-to-all-start.9 = ((bf16[8,136,544]{2,1,0:T(8,128)(2,1)}), bf16[8,136,544]{2,1,0:T(8,128)(2,1)S(1)}, u32[]{:S(2)}, u32[]{:S(2)}) async-start(bf16[8,136,544]{2,1,0:T(8,128)(2,1)} %bitcast.48), calls=%async_computation.9 | async-start | bytes 2785280 | tf_op jit(solution)/shard_map/all_to_all | solution.py:273
  213.7 167.3 %all-gather.15.cloned.1.call-start = ((), (), s32[]{:S(2)}) async-start(), calls=%async_computation.15 | async-start | bytes 2506752 | tf_op jit(solution)/shard_map/all_gather | solution.py:57
  235.7 1.1 copy-start.2
  236.7 36.2 %all-to-all-start.3 = ((bf16[8,128,1088]{1,2,0:T(8,128)(2,1)}), bf16[8,128,1088]{1,2,0:T(8,128)(2,1)}, u32[]{:S(2)}, u32[]{:S(2)}) async-start(bf16[8,128,1088]{1,2,0:T(8,128)(2,1)} %bitcast.155), calls=%async_computation.3 | async-start | bytes 4456448 | tf_op jit(solution)/shard_map/all_to_all | solution.py:61
  241.1 195.5 %all-reduce.14.cloned.1.call-start = ((), (), s32[]{:S(2)}) async-start(), calls=%async_computation.18 | async-start | bytes 4874240 | tf_op jit(solution)/shard_map/psum | solution.py:276
  244.9 30.6 %copy-start.5 = (bf16[1,128,1088]{1,2,0:T(8,128)(2,1)S(1)}, bf16[1,128,1088]{1,2,0:T(8,128)(2,1)}, u32[]{:S(2)}) copy-start(bf16[1,128,1088]{1,2,0:T(8,128)(2,1)} %param.15) | copy-start | bytes 835588
  274.9 1.7 copy-start.1
  276.6 1.6 copy-start.22
  276.6 1.9 copy-start.25
  316.1 7.5 %copy-start.9 = (bf16[128,320]{0,1:T(8,128)(2,1)S(1)}, bf16[128,320]{0,1:T(8,128)(2,1)}, u32[]{:S(2)}) copy-start(bf16[128,320]{0,1:T(8,128)(2,1)} %copy-done.8) | copy-start | bytes 245764
  316.1 7.5 %copy-start.11 = (bf16[128,320]{0,1:T(8,128)(2,1)S(1)}, bf16[128,320]{0,1:T(8,128)(2,1)}, u32[]{:S(2)}) copy-start(bf16[128,320]{0,1:T(8,128)(2,1)} %copy-done.10) | copy-start | bytes 245764
  316.1 7.5 %copy-start.13 = (bf16[128,320]{0,1:T(8,128)(2,1)S(1)}, bf16[128,320]{0,1:T(8,128)(2,1)}, u32[]{:S(2)}) copy-start(bf16[128,320]{0,1:T(8,128)(2,1)} %copy-done.12) | copy-start | bytes 245764
  316.1 7.5 %copy-start.15 = (bf16[128,320]{0,1:T(8,128)(2,1)S(1)}, bf16[128,320]{0,1:T(8,128)(2,1)}, u32[]{:S(2)}) copy-start(bf16[128,320]{0,1:T(8,128)(2,1)} %copy-done.14) | copy-start | bytes 245764
  318.4 35.9 %all-to-all-start.5 = ((bf16[4,128,960]{1,2,0:T(8,128)(2,1)}), bf16[4,128,960]{1,2,0:T(8,128)(2,1)}, u32[]{:S(2)}, u32[]{:S(2)}) async-start(bf16[4,128,960]{1,2,0:T(8,128)(2,1)} %copy.54), calls=%async_computation.5 | async-start | bytes 1966080 | tf_op jit(solution)/shard_map/all_to_all | solution.py:61
  322.7 132.0 %reduce-scatter.4.cloned.1.call-start = ((), (), s32[]{:S(2)}) async-start(), calls=%async_computation.16 | async-start | bytes 2820096
  323.6 2.3 copy-start.19
  375.9 17.7 %all-to-all-start.6 = ((bf16[128,8,408]{0,2,1:T(8,128)(2,1)}), bf16[128,8,408]{0,2,1:T(8,128)(2,1)S(1)}, u32[]{:S(2)}, u32[]{:S(2)}) async-start(bf16[128,8,408]{0,2,1:T(8,128)(2,1)} %bitcast.41), calls=%async_computation.6 | async-start | bytes 1671168 | tf_op jit(solution)/shard_map/all_to_all | solution.py:290
  428.5 88.6 %all-to-all-start.8 = ((bf16[8,128,1088]{1,2,0:T(8,128)(2,1)}), bf16[8,128,1088]{1,2,0:T(8,128)(2,1)}, u32[]{:S(2)}, u32[]{:S(2)}) async-start(bf16[8,128,1088]{1,2,0:T(8,128)(2,1)} %bitcast.154), calls=%async_computation.8 | async-start | bytes 4456448 | tf_op jit(solution)/shard_map/all_to_all | solution.py:61
  432.9 80.8 %all-reduce.12.cloned.1.call-start = ((), (), s32[]{:S(2)}) async-start(), calls=%async_computation.17 | async-start | bytes 2437120 | tf_op jit(solution)/shard_map/psum | solution.py:325
  458.1 16.1 %copy-start.7 = (bf16[136,4352]{1,0:T(8,128)(2,1)S(1)}, bf16[136,4352]{1,0:T(8,128)(2,1)}, u32[]{:S(2)}) copy-start(bf16[136,4352]{1,0:T(8,128)(2,1)} %get-tuple-element.58) | copy-start | bytes 3551236
  513.7 2.6 copy-start.16
  516.3 2.9 copy-start.17
Sparse Core Ops, SparseCore 0:
  9.9 52.1 all-gather.6
  64.0 29.4 all-gather.8
  95.4 28.6 all-gather.10
  171.9 25.9 all-gather.12
  216.6 37.0 all-gather.14
  281.3 118.7 all-reduce.13
  404.1 50.4 reduce-scatter.3
  457.1 56.5 all-reduce.11
